TPU v7x, 512 devices: a whole 4x4x16 slice. The times are simulated.
512 devices in a mesh: space: 64 (over z, y), dp: 8 (over x, core).
Axes of the slice: x: 4, y: 4, z: 16, core: 2. Of those that a mesh axis runs over, the one named last changes fastest.
Arguments:
- features: bfloat16 [8, 256, 4096], P('dp', 'space'), may hold values from -6 to 6
- sources: int32 [8, 256, 27], P('dp', 'space'), may hold values from 0 to 255, as said below
- voxels: int32 [8, 256, 1728], P('dp', 'space'), may hold values from 0 to 64, as said below
- cotangent: bfloat16 [8, 256, 4096], P('dp', 'space'), may hold values from -6 to 6
- weight_one: bfloat16 [27, 64, 64], replicated, may hold values from -0.15625 to 0.15625
- weight_two: bfloat16 [27, 64, 64], replicated, may hold values from -0.15625 to 0.15625
Outputs:
- conv_out: bfloat16 [8, 256, 4096], P('dp', 'space')
- grad_input: bfloat16 [8, 256, 4096], P('dp', 'space')
- grad_one: float32 [27, 64, 64], replicated
- grad_two: float32 [27, 64, 64], replicated
Inputs may be any that keep to these rules, and one draw needn't show every extreme that they name: `sources`: block b lies in slab b // 4. Each source block lies in the reader's own slab, or among the last 2 blocks of the slab before, or among the first 2 blocks of the slab after; every such boundary block is read by the neighbouring slab. Offset 27 // 2 reads the block itself. `voxels`: offset 27 // 2 maps every voxel to itself; the value 64 marks a voxel with no neighbour at that offset.
All inputs are finite; a program needn't handle non-finite values.
Results may differ from a plain program's by a relative error of at most 0.009.
Values may be sent and summed in bfloat16 or wider, within the bound.
A program may use at most 64 MiB of HBM per device.

v0:
```python
import jax
import jax.numpy as jnp
from jax import lax
from jax.sharding import Mesh
from jax.sharding import PartitionSpec as P

C = 64
V = 64
K = 27
HALO = 2
SPACE = ("space_0", "space_1")


def padded(cells, sides, width):
    for axis, dim in sides:
        count = lax.axis_size(axis)
        ends = count - 1
        head = lax.slice_in_dim(cells, 0, width, axis=dim)
        tail = lax.slice_in_dim(cells, cells.shape[dim] - width, cells.shape[dim], axis=dim)
        cells = jnp.concatenate(
            [
                lax.ppermute(tail, axis, [(i, (i + 1) % count) for i in range(ends)]),
                cells,
                lax.ppermute(head, axis, [((i + 1) % count, i) for i in range(ends)]),
            ],
            axis=dim,
        )
    return cells


def passed_along(block, axis, distance):
    devices = range(lax.axis_size(axis))
    route = [(i - distance, i) for i in devices if i - distance in devices]
    return lax.ppermute(block, axis, route)


def cut_along(x, dim, peers):
    dims = x.shape
    blocks = x.reshape(*dims[:dim], peers, dims[dim] // peers, *dims[dim + 1 :])
    return jnp.moveaxis(blocks, dim, 0)


def sent_and_summed(x, axis, dim):
    peers = lax.axis_size(axis)
    blocks = lax.all_to_all(cut_along(x, dim, peers), axis, 0, 0, tiled=True)
    return jnp.sum(blocks, axis=0)


def copy_for_each(x, axis):
    peers = lax.axis_size(axis)
    return lax.all_to_all(jnp.broadcast_to(x[None], (peers, *x.shape)), axis, 0, 0, tiled=True)


def taken_together(x, axis):
    everything = copy_for_each(x, axis)
    return jnp.sum(everything, axis=0)


def whole_of(x, axes, dim):
    for axis in reversed(axes):
        x = lax.all_gather(x, axis, axis=dim, tiled=True)
    return x


def pad_table(field, count):
    shaped = field.reshape(count, V, C)
    shaped = jnp.pad(shaped, ((0, 0), (0, 1), (0, 0)))
    return shaped.reshape(count * (V + 1), C)


def strip_table(table, count):
    return table.reshape(count, V + 1, C)[:, :V].reshape(count, V * C)


def conv_forward(table, rows, weight):
    picked = jnp.take(table, rows, axis=0)
    return jnp.einsum("knc,kcd->nd", picked, weight, preferred_element_type=jnp.float32)


def conv_backward(table, rows, weight, grad):
    picked = jnp.take(table, rows, axis=0)
    wgrads = jnp.einsum("knc,nd->kcd", picked, grad, preferred_element_type=jnp.float32)
    back = jnp.einsum("nd,kcd->knc", grad, weight, preferred_element_type=jnp.float32)
    start = jnp.zeros((table.shape[0], C), jnp.float32)
    accum = start.at[rows.reshape(-1)].add(back.reshape(-1, C))
    return (wgrads, accum)


def slope(pre):
    sig = jax.nn.sigmoid(pre)
    return sig * (1.0 + pre * (1.0 - sig))


def extend(field):
    return padded(field, ((SPACE, 0),), HALO)


def return_rims(accum, blocks):
    wide = strip_table(accum, blocks + 2 * HALO)
    lower = wide[:HALO]
    own = wide[HALO : HALO + blocks]
    upper = wide[HALO + blocks :]
    from_after = passed_along(lower.astype(jnp.bfloat16), SPACE, -1).astype(lower.dtype)
    from_before = passed_along(upper.astype(jnp.bfloat16), SPACE, 1).astype(upper.dtype)
    own = own.at[blocks - HALO :].add(from_after)
    own = own.at[:HALO].add(from_before)
    return own


def per_device(features, sources, voxels, cotangent, weight_one, weight_two):
    blocks = features.shape[1]
    wide_count = blocks + 2 * HALO
    me = lax.axis_index(SPACE)
    feat = features[0]
    source_ids = sources[0]
    owner = source_ids // blocks
    place = source_ids % blocks
    slot = jnp.where(
        owner == me,
        HALO + place,
        jnp.where(owner < me, place - (blocks - HALO), HALO + blocks + place),
    )
    vox = voxels[0].reshape(blocks, K, V)
    rows = slot[:, :, None] * (V + 1) + vox
    rows = jnp.transpose(rows, (1, 0, 2)).reshape(K, blocks * V)
    table_in = pad_table(extend(feat), wide_count)
    pre = conv_forward(table_in, rows, weight_one)
    hidden = jax.nn.silu(pre).astype(jnp.bfloat16).reshape(blocks, V * C)
    table_hidden = pad_table(extend(hidden), wide_count)
    conv_out = conv_forward(table_hidden, rows, weight_two).astype(jnp.bfloat16)
    grad_out = cotangent[0].reshape(blocks * V, C)
    part_two, back_hidden = conv_backward(table_hidden, rows, weight_two, grad_out)
    grad_hidden = return_rims(back_hidden, blocks).reshape(blocks * V, C)
    grad_pre = (grad_hidden * slope(pre)).astype(jnp.bfloat16)
    part_one, back_in = conv_backward(table_in, rows, weight_one, grad_pre)
    grad_input = return_rims(back_in, blocks).astype(jnp.bfloat16)
    factor = float(lax.axis_size("dp") * lax.axis_size(SPACE) * blocks * V) ** (-0.5)
    flat = jnp.concatenate([part_one.reshape(-1), part_two.reshape(-1)])
    share = sent_and_summed(flat, SPACE, 0)
    share = taken_together(share, "dp")
    whole = whole_of(share, SPACE, 0)
    total_one = whole[: K * C * C].reshape(K, C, C)
    total_two = whole[K * C * C :].reshape(K, C, C)
    out_block = conv_out.reshape(1, blocks, V * C)
    grad_block = grad_input.reshape(1, blocks, V * C)
    return (out_block, grad_block, total_one * factor, total_two * factor)


def solution(mesh):
    finer = Mesh(mesh.devices.reshape(16, 4, mesh.shape["dp"]), ("space_0", "space_1", "dp"))
    in_specs = (
        P("dp", SPACE, None),
        P("dp", SPACE, None),
        P("dp", SPACE, None),
        P("dp", SPACE, None),
        P(),
        P(),
    )
    out_specs = (P("dp", SPACE, None), P("dp", SPACE, None), P(), P())
    return jax.shard_map(
        per_device, mesh=finer, in_specs=in_specs, out_specs=out_specs, check_vma=False
    )
```

profile of v0, /device:TPU:32, one launch (start us, length us, event | category | flops | bytes accessed | tf_op | source)
XLA Modules:
  0.0 251.7 jit_solution(8718744548756460276)
XLA Ops:
  0.6 0.9 slice_bitcast_fusion.1
  1.5 3.5 %collective-permute-start = (bf16[2,4096]{1,0:T(2,128)(2,1)S(1)}, bf16[2,4096]{1,0:T(2,128)(2,1)S(1)}, u32[]{:S(2)}, u32[]{:S(2)}) collective-permute-start(bf16[2,4096]{1,0:T(2,128)(2,1)S(1)} %get-tuple-element.63), channel_id=1, source_target_pairs={{0,8},{8,16},{16,24},{24,32},{32,40},{40,48},{48,56},{56,64},{64,7... | collective-permute-start | bytes 49160 | tf_op jit(solution)/shard_map/ppermute | solution.py:22
  5.0 4.5 %collective-permute-start.1 = (bf16[2,4096]{1,0:T(2,128)(2,1)S(1)}, bf16[2,4096]{1,0:T(2,128)(2,1)S(1)}, u32[]{:S(2)}, u32[]{:S(2)}) collective-permute-start(bf16[2,4096]{1,0:T(2,128)(2,1)S(1)} %get-tuple-element.64), channel_id=1, source_target_pairs={{8,0},{16,8},{24,16},{32,24},{40,32},{48,40},{56,48},{64,56},{72,6... | collective-permute-start | bytes 49160 | tf_op jit(solution)/shard_map/ppermute | solution.py:24
  9.5 0.9 reshape_squeeze.7
  10.4 0.9 reshape_squeeze.6
  11.2 0.7 select_multiply_fusion
  12.1 0.1 reshape_reshape.4
  12.3 1.4 convolution_bitcast_fusion.1
  13.7 2.5 copy.176
  16.2 39.1 %scatter_custom_fusion = f32[520,64]{1,0:T(8,128)S(1)} fusion(s32[6912]{0:T(1024)S(1)} %fusion.29, f32[6912,64]{1,0:T(8,128)} %bitcast.69, f32[]{:T(128)} %constant.162.clone.1), kind=kCustom, calls=%fused_computation.32 | custom fusion | flops 442368 | bytes 133632 | tf_op jit(solution)/shard_map/scatter-add | solution.py:85
  55.3 0.1 copy.156
  55.4 0.1 reshape.298
  55.8 1.9 collective-permute-start.5
  58.0 6.0 %collective-permute-start.4 = (bf16[2,4096]{1,0:T(2,128)(2,1)S(1)}, bf16[2,4096]{1,0:T(2,128)(2,1)S(1)}, u32[]{:S(2)}, u32[]{:S(2)}) collective-permute-start(bf16[2,4096]{1,0:T(2,128)(2,1)S(1)} %convert_element_type.45), channel_id=1, source_target_pairs={{8,0},{16,8},{24,16},{32,24},{40,32},{48,40},{56,48},{64,56},{72,6... | collective-permute-start | bytes 49160 | tf_op jit(solution)/shard_map/ppermute | solution.py:34
  64.2 0.1 concatenate.37
  64.4 0.1 copy.139
  64.8 0.1 slice.175
  65.5 0.2 fusion.22
  65.6 0.1 reshape.293
  65.8 0.1 copy.141
  65.9 13.0 %gather_fusion = bf16[6912,64]{1,0:T(8,128)(2,1)S(1)} fusion(bf16[520,64]{1,0:T(8,128)(2,1)S(1)} %copy.141, s32[7168]{0:T(1024)S(1)} %pad_clamp_fusion), kind=kCustom, calls=%fused_computation.clone | custom fusion | bytes 1797120 | tf_op jit(solution)/shard_map/jit(_take)/gather | solution.py:76
  79.0 0.9 copy.142
  79.9 0.1 reshape.300
  80.1 0.3 convolution_bitcast_fusion.3
  80.5 0.1 copy.144
  80.6 0.1 slice.171
  80.8 1.9 collective-permute-start.2
  82.7 0.1 copy.145
  82.8 0.1 slice.173
  82.9 6.3 %collective-permute-start.3 = (bf16[2,4096]{1,0:T(2,128)(2,1)S(1)}, bf16[2,4096]{1,0:T(2,128)(2,1)S(1)}, u32[]{:S(2)}, u32[]{:S(2)}) collective-permute-start(bf16[2,4096]{1,0:T(2,128)(2,1)S(1)} %slice.173), channel_id=1, source_target_pairs={{8,0},{16,8},{24,16},{32,24},{40,32},{48,40},{56,48},{64,56},{72,6... | collective-permute-start | bytes 49160 | tf_op jit(solution)/shard_map/ppermute | solution.py:24
  89.2 0.4 fusion.2
  89.7 0.2 concatenate.44
  90.2 0.5 collective-permute-done.3
  90.9 0.2 fusion.20
  91.0 0.1 reshape.295
  91.2 0.1 copy.148
  91.3 13.0 %gather_fusion.1 = bf16[6912,64]{1,0:T(8,128)(2,1)S(1)} fusion(bf16[520,64]{1,0:T(8,128)(2,1)S(1)} %copy.148, s32[7168]{0:T(1024)S(1)} %copy-done.6), kind=kCustom, calls=%fused_computation.1.clone | custom fusion | bytes 1797120 | tf_op jit(solution)/shard_map/jit(_take)/gather | solution.py:76
  104.4 0.9 copy.149
  105.2 1.3 fusion.1
  106.6 0.2 concatenate.45
  106.9 1.5 all_to_all.10
  108.4 22.3 %all-to-all-start = ((f32[64,1,3456]{2,1,0:T(1,128)}), f32[64,1,3456]{2,1,0:T(1,128)S(1)}, u32[]{:S(2)}, u32[]{:S(2)}) async-start(f32[64,1,3456]{2,1,0:T(1,128)} %all_to_all.10), calls=%async_computation | async-start | bytes 1769472 | tf_op jit(solution)/shard_map/all_to_all | solution.py:45
  130.8 0.4 convolution_bitcast_fusion
  131.1 2.5 copy.177
  133.6 39.1 %scatter_custom_fusion.1 = f32[520,64]{1,0:T(8,128)S(1)} fusion(s32[6912]{0:T(1024)} %copy-done.10, f32[6912,64]{1,0:T(8,128)} %bitcast.68, f32[]{:T(128)} %constant.162.clone.1), kind=kCustom, calls=%fused_computation.30 | custom fusion | flops 442368 | bytes 133632 | tf_op jit(solution)/shard_map/scatter-add | solution.py:85
  172.7 0.1 copy.164
  172.8 0.1 reshape.302
  173.3 4.7 %collective-permute-start.6 = (bf16[2,4096]{1,0:T(2,128)(2,1)S(1)}, bf16[2,4096]{1,0:T(2,128)(2,1)S(1)}, u32[]{:S(2)}, u32[]{:S(2)}) collective-permute-start(bf16[2,4096]{1,0:T(2,128)(2,1)S(1)} %convert_element_type.50), channel_id=1, source_target_pairs={{8,0},{16,8},{24,16},{32,24},{40,32},{48,40},{56,48},{64,56},{72,6... | collective-permute-start | bytes 49160 | tf_op jit(solution)/shard_map/ppermute | solution.py:34
  178.6 0.1 slice.181
  178.7 1.9 collective-permute-start.7
  180.7 5.8 %collective-permute-done.7 = bf16[2,4096]{1,0:T(2,128)(2,1)S(1)} collective-permute-done((bf16[2,4096]{1,0:T(2,128)(2,1)S(1)}, bf16[2,4096]{1,0:T(2,128)(2,1)S(1)}, u32[]{:S(2)}, u32[]{:S(2)}) %collective-permute-start.7) | collective-permute-done | bytes 16416 | tf_op jit(solution)/shard_map/ppermute | solution.py:34
  186.5 0.6 convert_bitcast_fusion
  187.1 0.5 reduce_sum.18
  187.6 0.7 broadcast_in_dim.11
  188.3 4.3 %all-to-all-start.1 = ((f32[8,1,3456]{2,1,0:T(1,128)}), f32[8,1,3456]{2,1,0:T(1,128)S(1)}, u32[]{:S(2)}, u32[]{:S(2)}) async-start(f32[8,1,3456]{2,1,0:T(1,128)} %broadcast_in_dim.11), calls=%async_computation.1 | async-start | bytes 221184 | tf_op jit(solution)/shard_map/all_to_all | solution.py:51
  192.6 0.3 fusion
  193.0 0.1 copy.151
  193.1 0.7 reshape.296
  193.8 4.7 %all-to-all-done.1 = f32[8,1,3456]{2,1,0:T(1,128)S(1)} async-done(((f32[8,1,3456]{2,1,0:T(1,128)}), f32[8,1,3456]{2,1,0:T(1,128)S(1)}, u32[]{:S(2)}, u32[]{:S(2)}) %all-to-all-start.1) | async-done | bytes 110624 | tf_op jit(solution)/shard_map/all_to_all | solution.py:51
  198.6 11.9 %all-gather = f32[4,1,3456]{2,1,0:T(1,128)S(1)} all-gather(f32[1,1,3456]{2,1,0:T(1,128)S(1)} %reshape.341), channel_id=1, replica_groups=mesh['space_0'=16,'space_1'=4,'dp'=8] {'space_1'}, dimensions={0}, use_global_device_ids=true | all-gather | bytes 69120 | tf_op jit(solution)/shard_map/all_gather | solution.py:61
  210.5 36.5 %all-gather.1 = f32[16,1,13824]{2,1,0:T(1,128)S(1)} all-gather(f32[1,1,13824]{2,1,0:T(1,128)S(1)} %bitcast.70), channel_id=1, replica_groups=mesh['space_0'=16,'space_1'=4,'dp'=8] {'space_0'}, dimensions={0}, use_global_device_ids=true | all-gather | bytes 940032 | tf_op jit(solution)/shard_map/all_gather | solution.py:61
  247.0 2.5 %fusion.3 = (f32[8,13824]{1,0:T(8,128)S(1)}, f32[8,13824]{1,0:T(8,128)S(1)}) fusion(f32[16,1,13824]{2,1,0:T(1,128)S(1)} %all-gather.1), kind=kLoop, calls=%fused_computation.15 | loop fusion | flops 221184 | bytes 1769472 | tf_op jit(solution)/shard_map/mul | solution.py:146
  249.5 1.1 mul.49
  250.6 1.1 mul.47
  (78 shorter events, 3.4 us)
Async XLA Ops:
  0.6 79.5 %copy-start = (bf16[27,64,64]{2,1,0:T(8,128)(2,1)S(1)}, bf16[27,64,64]{2,1,0:T(8,128)(2,1)}, u32[]{:S(2)}) copy-start(bf16[27,64,64]{2,1,0:T(8,128)(2,1)} %param.20) | copy-start | bytes 663556
  1.5 63.4 %collective-permute-start = (bf16[2,4096]{1,0:T(2,128)(2,1)S(1)}, bf16[2,4096]{1,0:T(2,128)(2,1)S(1)}, u32[]{:S(2)}, u32[]{:S(2)}) collective-permute-start(bf16[2,4096]{1,0:T(2,128)(2,1)S(1)} %get-tuple-element.63), channel_id=1, source_target_pairs={{0,8},{8,16},{16,24},{24,32},{32,40},{40,48},{48,56},{56,64},{64,7... | collective-permute-start | bytes 49160 | tf_op jit(solution)/shard_map/ppermute | solution.py:22
  5.0 60.1 %collective-permute-start.1 = (bf16[2,4096]{1,0:T(2,128)(2,1)S(1)}, bf16[2,4096]{1,0:T(2,128)(2,1)S(1)}, u32[]{:S(2)}, u32[]{:S(2)}) collective-permute-start(bf16[2,4096]{1,0:T(2,128)(2,1)S(1)} %get-tuple-element.64), channel_id=1, source_target_pairs={{8,0},{16,8},{24,16},{32,24},{40,32},{48,40},{56,48},{64,56},{72,6... | collective-permute-start | bytes 49160 | tf_op jit(solution)/shard_map/ppermute | solution.py:24
  10.4 5.8 %copy-start.3 = (bf16[256,64]{1,0:T(8,128)(2,1)}, bf16[256,64]{1,0:T(8,128)(2,1)S(1)}, u32[]{:S(2)}) copy-start(bf16[256,64]{1,0:T(8,128)(2,1)S(1)} %reshape_squeeze.7) | copy-start | bytes 98308
  12.3 3.9 %copy-start.10 = (s32[6912]{0:T(1024)}, s32[6912]{0:T(1024)S(1)}, u32[]{:S(2)}) copy-start(s32[6912]{0:T(1024)S(1)} %fusion.29) | copy-start | bytes 82948
  16.2 48.0 %copy-start.9 = (bf16[1,4,4096]{2,1,0:T(4,128)(2,1)S(1)}, bf16[1,4,4096]{2,1,0:T(4,128)(2,1)}, u32[]{:S(2)}) copy-start(bf16[1,4,4096]{2,1,0:T(4,128)(2,1)} %param.16) | copy-start | bytes 98308
  55.8 24.0 %collective-permute-start.5 = (bf16[2,4096]{1,0:T(2,128)(2,1)S(1)}, bf16[2,4096]{1,0:T(2,128)(2,1)S(1)}, u32[]{:S(2)}, u32[]{:S(2)}) collective-permute-start(bf16[2,4096]{1,0:T(2,128)(2,1)S(1)} %convert_element_type.47), channel_id=1, source_target_pairs={{0,8},{8,16},{16,24},{24,32},{32,40},{40,48},{48,56},{56,64},{64,7... | collective-permute-start | bytes 49160 | tf_op jit(solution)/shard_map/ppermute | solution.py:34
  58.0 7.5 %collective-permute-start.4 = (bf16[2,4096]{1,0:T(2,128)(2,1)S(1)}, bf16[2,4096]{1,0:T(2,128)(2,1)S(1)}, u32[]{:S(2)}, u32[]{:S(2)}) collective-permute-start(bf16[2,4096]{1,0:T(2,128)(2,1)S(1)} %convert_element_type.45), channel_id=1, source_target_pairs={{8,0},{16,8},{24,16},{32,24},{40,32},{48,40},{56,48},{64,56},{72,6... | collective-permute-start | bytes 49160 | tf_op jit(solution)/shard_map/ppermute | solution.py:34
  64.2 14.8 %copy-start.5 = (s32[7168]{0:T(1024)}, s32[7168]{0:T(1024)S(1)}, u32[]{:S(2)}) copy-start(s32[7168]{0:T(1024)S(1)} %pad_clamp_fusion) | copy-start | bytes 86020
  80.5 9.6 %copy-start.7 = (bf16[256,64]{0,1:T(8,128)(2,1)}, bf16[256,64]{0,1:T(8,128)(2,1)S(1)}, u32[]{:S(2)}) copy-start(bf16[256,64]{0,1:T(8,128)(2,1)S(1)} %get-tuple-element.59) | copy-start | bytes 98308
  80.8 9.2 %collective-permute-start.2 = (bf16[2,4096]{1,0:T(2,128)(2,1)S(1)}, bf16[2,4096]{1,0:T(2,128)(2,1)S(1)}, u32[]{:S(2)}, u32[]{:S(2)}) collective-permute-start(bf16[2,4096]{1,0:T(2,128)(2,1)S(1)} %slice.171), channel_id=1, source_target_pairs={{0,8},{8,16},{16,24},{24,32},{32,40},{40,48},{48,56},{56,64},{64,7... | collective-permute-start | bytes 49160 | tf_op jit(solution)/shard_map/ppermute | solution.py:22
  82.9 7.7 %collective-permute-start.3 = (bf16[2,4096]{1,0:T(2,128)(2,1)S(1)}, bf16[2,4096]{1,0:T(2,128)(2,1)S(1)}, u32[]{:S(2)}, u32[]{:S(2)}) collective-permute-start(bf16[2,4096]{1,0:T(2,128)(2,1)S(1)} %slice.173), channel_id=1, source_target_pairs={{8,0},{16,8},{24,16},{32,24},{40,32},{48,40},{56,48},{64,56},{72,6... | collective-permute-start | bytes 49160 | tf_op jit(solution)/shard_map/ppermute | solution.py:24
  89.6 1.7 copy-start.6
  105.2 1.6 copy-start.1
  106.9 23.9 %copy-start.8 = (bf16[256,64]{0,1:T(8,128)(2,1)S(1)}, bf16[256,64]{0,1:T(8,128)(2,1)}, u32[]{:S(2)}) copy-start(bf16[256,64]{0,1:T(8,128)(2,1)} %copy-done.7) | copy-start | bytes 98308
  108.4 78.7 %all-to-all-start = ((f32[64,1,3456]{2,1,0:T(1,128)}), f32[64,1,3456]{2,1,0:T(1,128)S(1)}, u32[]{:S(2)}, u32[]{:S(2)}) async-start(f32[64,1,3456]{2,1,0:T(1,128)} %all_to_all.10), calls=%async_computation | async-start | bytes 1769472 | tf_op jit(solution)/shard_map/all_to_all | solution.py:45
  173.0 19.6 %copy-start.2 = (bf16[27,256,64]{1,2,0:T(8,128)(2,1)S(1)}, bf16[27,256,64]{1,2,0:T(8,128)(2,1)}, u32[]{:S(2)}) copy-start(bf16[27,256,64]{1,2,0:T(8,128)(2,1)} %copy-done.1) | copy-start | bytes 2654212
  173.0 19.6 %copy-start.4 = (bf16[27,64,64]{2,1,0:T(8,128)(2,1)S(1)}, bf16[27,64,64]{2,1,0:T(8,128)(2,1)}, u32[]{:S(2)}) copy-start(bf16[27,64,64]{2,1,0:T(8,128)(2,1)} %param.21) | copy-start | bytes 663556
  173.3 7.3 %collective-permute-start.6 = (bf16[2,4096]{1,0:T(2,128)(2,1)S(1)}, bf16[2,4096]{1,0:T(2,128)(2,1)S(1)}, u32[]{:S(2)}, u32[]{:S(2)}) collective-permute-start(bf16[2,4096]{1,0:T(2,128)(2,1)S(1)} %convert_element_type.50), channel_id=1, source_target_pairs={{8,0},{16,8},{24,16},{32,24},{40,32},{48,40},{56,48},{64,56},{72,6... | collective-permute-start | bytes 49160 | tf_op jit(solution)/shard_map/ppermute | solution.py:34
  178.7 7.7 %collective-permute-start.7 = (bf16[2,4096]{1,0:T(2,128)(2,1)S(1)}, bf16[2,4096]{1,0:T(2,128)(2,1)S(1)}, u32[]{:S(2)}, u32[]{:S(2)}) collective-permute-start(bf16[2,4096]{1,0:T(2,128)(2,1)S(1)} %convert_element_type.52), channel_id=1, source_target_pairs={{0,8},{8,16},{16,24},{24,32},{32,40},{40,48},{48,56},{56,64},{64,7... | collective-permute-start | bytes 49160 | tf_op jit(solution)/shard_map/ppermute | solution.py:34
  188.3 10.2 %all-to-all-start.1 = ((f32[8,1,3456]{2,1,0:T(1,128)}), f32[8,1,3456]{2,1,0:T(1,128)S(1)}, u32[]{:S(2)}, u32[]{:S(2)}) async-start(f32[8,1,3456]{2,1,0:T(1,128)} %broadcast_in_dim.11), calls=%async_computation.1 | async-start | bytes 221184 | tf_op jit(solution)/shard_map/all_to_all | solution.py:51
where the time goes:
time: 253 us; the launch traced here: 252 us
  other arithmetic  83.4 us (33%)
  starting transfers between devices  57.4 us (23%)
  blocking collectives  48.4 us (19%)
  local copies, waits for them, and re-layouts  46.1 us (18%)
  waiting for transfers between devices  11 us (4%)
  matrix products  4.08 us (2%)
    scatter-add x2, other arithmetic, conv_backward(): accum = start.at[rows.reshape(-1)].add(back.reshape(-1, C))  78.1 us
    all_gather x2, blocking collectives, whole_of(): x = lax.all_gather(x, axis, axis=dim, tiled=True)  48.4 us
    gather x4, local copies, waits for them, and re-layouts, conv_forward(): picked = jnp.take(table, rows, axis=0)  27.8 us
    all_to_all x1, starting transfers between devices, sent_and_summed(): blocks = lax.all_to_all(cut_along(x, dim, peers), axis, 0, 0, tiled=True)  22.3 us
    ppermute x4, starting transfers between devices, passed_along(): return lax.ppermute(block, axis, route)  14.6 us
    ppermute x2, starting transfers between devices, padded(): lax.ppermute(head, axis, [((i + 1) % count, i) for i in range(ends)])  10.8 us
    ppermute x4, waiting for transfers between devices, passed_along(): return lax.ppermute(block, axis, route)  5.85 us
    ppermute x2, starting transfers between devices, padded(): lax.ppermute(tail, axis, [(i, (i + 1) % count) for i in range(ends)])  5.41 us
  transfers between devices with their start and end apart: 10, of which 4 were waited for; matrix products, arithmetic and copies ran while one was open for 43% of the time, Pallas kernels for 0%

commit v1 on v0

v1 whole, which is shorter than its diff:
```python
import functools

import jax
import jax.numpy as jnp
from jax import lax
from jax.experimental import pallas as pl
from jax.experimental.pallas import tpu as pltpu
from jax.sharding import PartitionSpec as P

C = 64
V = 64
K = 27
HALO = 2
Y = 4
ZPAR = 2
TILE = 16
TILES = K * C * C // (TILE * 2 * C)
MESH = pl.DeviceIdType.MESH
BF16 = jnp.bfloat16
F32 = jnp.float32


def mxu(a, b, dims=((1,), (0,))):
    return lax.dot_general(a, b, (dims, ((), ())), preferred_element_type=F32)


def step_kernel(
    sizes,
    feat_ref,
    cot_ref,
    rows_ref,
    w1_ref,
    w2_ref,
    conv_ref,
    gin_ref,
    sums_ref,
    hots,
    picked1,
    picked2,
    back,
    w1t,
    w2t,
    halo_in,
    halo_mid,
    rim_out,
    rim_in,
    hidden,
    parts,
    got1,
    mid,
    got2,
    got3,
    whole2,
    halo_send,
    halo_recv,
    group_send,
    group_recv,
):
    space, dp, planes, deep = sizes
    n = feat_ref.shape[1]
    half = n // 2
    t1 = parts.shape[1] // dp
    t2 = mid.shape[1] // planes
    s = lax.axis_index("space")
    d = lax.axis_index("dp")
    y = s % Y
    z = s // Y
    plane = (z % ZPAR) * Y + y
    depth = z // ZPAR

    def at_dp(i):
        return (s, i)

    def at_plane(i):
        return (((z // ZPAR) * ZPAR + i // Y) * Y + i % Y, d)

    def at_depth(i):
        return ((i * ZPAR + z % ZPAR) * Y + y, d)

    before = ((s + space - 1) % space, d)
    after = ((s + 1) % space, d)

    barrier = pltpu.get_barrier_semaphore()
    partners = [before, after]
    for group, me, at in ((dp, d, at_dp), (planes, plane, at_plane), (deep, depth, at_depth)):
        partners += [at((me + j) % group) for j in range(1, group)]
    for partner in partners:
        pl.semaphore_signal(barrier, inc=1, device_id=partner, device_id_type=MESH)

    def remote(src, dst, send, recv, target):
        return pltpu.make_async_remote_copy(
            src_ref=src, dst_ref=dst, send_sem=send, recv_sem=recv, device_id=target, device_id_type=MESH
        )

    spot = lax.broadcasted_iota(jnp.int32, (2 * n, n), 0)

    def build(k, carry):
        row = rows_ref[k]
        hot = jnp.where(spot == row, 1.0, 0.0).astype(BF16)
        hots[:, pl.ds(pl.multiple_of(k * n, n), n)] = hot
        return carry

    lax.fori_loop(0, K, build, 0)

    group_of = 9

    def spread(w_ref, grad):
        for g in range(0, K, group_of):
            out = mxu(w_ref[g * C : (g + group_of) * C, :], grad).astype(BF16)
            for k in range(group_of):
                back[:, (g + k) * n : (g + k + 1) * n] = out[k * C : (k + 1) * C, :]

    def scattered(lo, hi):
        def some(g, total):
            lanes = pl.ds(pl.multiple_of(g * group_of * n, group_of * n), group_of * n)
            return total + mxu(back[:, lanes], hots[lo:hi, lanes], ((1,), (1,)))

        return lax.fori_loop(0, K // group_of, some, jnp.zeros((C, hi - lo), F32))

    def pick_own(table, picked):
        def one(g, carry):
            for i in range(group_of):
                k = g * group_of + i
                lanes = pl.ds(pl.multiple_of(k * n, n), n)
                picked[k] = mxu(table, hots[0:n, lanes]).astype(BF16)
            return carry

        lax.fori_loop(0, K // group_of, one, 0)

    def pick_halo(table, picked):
        def one(g, carry):
            for i in range(group_of):
                k = g * group_of + i
                lanes = pl.ds(pl.multiple_of(k * n, n), n)
                more = mxu(table, hots[n : 2 * n, lanes])
                picked[k] = (picked[k].astype(F32) + more).astype(BF16)
            return carry

        lax.fori_loop(0, K // group_of, one, 0)

    def convolved(wt, picked):
        return mxu(wt[...], picked[...].reshape(K * C, n))

    def weight_parts(which, picked, grad):
        zero = jnp.zeros((C, n), BF16)
        pair = jnp.concatenate(
            [jnp.concatenate([grad, zero], axis=1), jnp.concatenate([zero, grad], axis=1)], axis=0
        )
        for g in range(0, K, group_of):
            both = jnp.concatenate(
                [picked[g : g + group_of, 0 : C // 2, :], picked[g : g + group_of, C // 2 : C, :]], axis=2
            ).reshape(group_of * C // 2, 2 * n)
            out = mxu(both, pair, ((1,), (1,))).astype(BF16)
            tiles = group_of * C // 2 // TILE
            parts[which, g * 2 : g * 2 + tiles] = out.reshape(tiles, TILE, 2 * C)

    def to_neighbours(slot, low, high, into):
        copies = [
            remote(low, into.at[1], halo_send.at[slot, 0], halo_recv.at[slot, 1], before),
            remote(high, into.at[0], halo_send.at[slot, 1], halo_recv.at[slot, 0], after),
        ]
        for copy in copies:
            copy.start()
        return copies

    def arrive(copies):
        for copy in copies:
            copy.wait_recv()

    def to_group(stage, which, group, me, at, src_of, dst):
        copies = []
        for j in range(1, group):
            other = (me + j) % group
            copy = remote(
                src_of(other),
                dst,
                group_send.at[stage, which, j - 1],
                group_recv.at[stage, which, j - 1],
                at(other),
            )
            copy.start()
            copies.append(copy)
        return copies

    feat = feat_ref[...]
    cot = cot_ref[...]
    w1t[...] = w1_ref[...].T
    w2t[...] = w2_ref[...].T
    for which in range(2):
        parts[which, TILES:] = jnp.zeros((parts.shape[1] - TILES, TILE, 2 * C), BF16)
        mid[which, t1:] = jnp.zeros((mid.shape[1] - t1, TILE, 2 * C), BF16)
    spread(w2_ref, cot)
    rim = scattered(n, 2 * n).astype(BF16)
    for i in range(2):
        rim_out[0, i] = rim[:, i * half : (i + 1) * half]

    pl.semaphore_wait(barrier, len(partners))

    sent = []
    feat_copies = to_neighbours(0, feat_ref.at[:, 0:half], feat_ref.at[:, half:n], halo_in)
    rim_copies = to_neighbours(1, rim_out.at[0, 0], rim_out.at[0, 1], rim_in.at[0])
    sent += feat_copies + rim_copies

    pick_own(feat, picked1)
    grad_hidden = scattered(0, n)

    arrive(feat_copies)
    pick_halo(jnp.concatenate([halo_in[0], halo_in[1]], axis=1), picked1)
    pre = convolved(w1t, picked1)
    sig = 1.0 / (1.0 + jnp.exp(-pre))
    hid = (pre * sig).astype(BF16)
    hidden[...] = hid
    hid_copies = to_neighbours(2, hidden.at[:, 0:half], hidden.at[:, half:n], halo_mid)
    sent += hid_copies

    arrive(rim_copies)
    rims = jnp.concatenate([rim_in[0, 0], rim_in[0, 1]], axis=1).astype(F32)
    grad_pre = ((grad_hidden + rims) * (sig * (1.0 + pre * (1.0 - sig)))).astype(BF16)
    weight_parts(0, picked1, grad_pre)

    def scatter_reduce_1(which):
        return to_group(
            0,
            which,
            dp,
            d,
            at_dp,
            lambda other: parts.at[which, pl.ds(other * t1, t1)],
            got1.at[which, d],
        )

    def scatter_reduce_2(which, copies):
        arrive(copies)
        got1[which, d] = parts[which, pl.ds(d * t1, t1)]
        total = got1[which, 0].astype(F32)
        for i in range(1, dp):
            total = total + got1[which, i].astype(F32)
        mid[which, 0:t1] = total.astype(BF16)
        return to_group(
            1,
            which,
            planes,
            plane,
            at_plane,
            lambda other: mid.at[which, pl.ds(other * t2, t2)],
            got2.at[which, plane],
        )

    def reduce_3(which, copies):
        arrive(copies)
        got2[which, plane] = mid[which, pl.ds(plane * t2, t2)]
        total = got2[which, 0].astype(F32)
        for i in range(1, planes):
            total = total + got2[which, i].astype(F32)
        got3[which, depth] = total.astype(BF16)
        return to_group(2, which, deep, depth, at_depth, lambda other: got3.at[which, depth], got3.at[which, depth])

    def gather_2(which, copies):
        arrive(copies)
        total = got3[which, 0].astype(F32)
        for i in range(1, deep):
            total = total + got3[which, i].astype(F32)
        mine = pl.ds(plane * t2, t2)
        whole2[which, mine] = total.astype(BF16)
        return to_group(
            3, which, planes, plane, at_plane, lambda other: whole2.at[which, mine], whole2.at[which, mine]
        )

    def gather_1(which, copies):
        arrive(copies)
        mine = whole2.at[which, 0:t1]
        sums_ref[which, d] = whole2[which, 0:t1]
        return to_group(4, which, dp, d, at_dp, lambda other: mine, sums_ref.at[which, d])

    one = scatter_reduce_1(0)
    sent += one

    pick_own(hid, picked2)
    arrive(hid_copies)
    pick_halo(jnp.concatenate([halo_mid[0], halo_mid[1]], axis=1), picked2)
    weight_parts(1, picked2, cot)
    two = scatter_reduce_1(1)
    sent += two

    spread(w1_ref, grad_pre)
    rim = scattered(n, 2 * n).astype(BF16)
    for i in range(2):
        rim_out[1, i] = rim[:, i * half : (i + 1) * half]
    last_copies = to_neighbours(3, rim_out.at[1, 0], rim_out.at[1, 1], rim_in.at[1])
    sent += last_copies

    one = scatter_reduce_2(0, one)
    sent += one
    conv_ref[...] = convolved(w2t, picked2).astype(BF16)
    two = scatter_reduce_2(1, two)
    sent += two
    one = reduce_3(0, one)
    sent += one
    grad_in = scattered(0, n)
    two = reduce_3(1, two)
    sent += two
    arrive(last_copies)
    rims = jnp.concatenate([rim_in[1, 0], rim_in[1, 1]], axis=1).astype(F32)
    gin_ref[...] = (grad_in + rims).astype(BF16)

    one = gather_2(0, one)
    sent += one
    two = gather_2(1, two)
    sent += two
    one = gather_1(0, one)
    sent += one
    two = gather_1(1, two)
    sent += two
    arrive(one)
    arrive(two)
    for copy in sent:
        copy.wait_send()


def per_device(sizes, features, sources, voxels, cotangent, weight_one, weight_two):
    space, dp, planes, deep = sizes
    blocks = features.shape[1]
    n = blocks * V
    half = n // 2
    me = lax.axis_index("space")
    source_ids = sources[0]
    owner = source_ids // blocks
    place = source_ids % blocks
    slot = jnp.where(owner == me, place, jnp.where(owner < me, place + HALO, blocks + HALO + place))
    vox = voxels[0].reshape(blocks, K, V)
    rows = jnp.where(vox == V, -1, slot[:, :, None] * V + vox)
    rows = jnp.transpose(rows, (1, 0, 2)).reshape(K, 1, n)
    feat = features[0].reshape(n, C).T
    cot = cotangent[0].reshape(n, C).T
    t1 = -(-TILES // dp)
    t2 = -(-t1 // planes)
    scratch = [
        pltpu.VMEM((2 * n, K * n), BF16),
        pltpu.VMEM((K, C, n), BF16),
        pltpu.VMEM((K, C, n), BF16),
        pltpu.VMEM((C, K * n), BF16),
        pltpu.VMEM((C, K * C), BF16),
        pltpu.VMEM((C, K * C), BF16),
        pltpu.VMEM((2, C, half), BF16),
        pltpu.VMEM((2, C, half), BF16),
        pltpu.VMEM((2, 2, C, half), BF16),
        pltpu.VMEM((2, 2, C, half), BF16),
        pltpu.VMEM((C, n), BF16),
        pltpu.VMEM((2, dp * t1, TILE, 2 * C), BF16),
        pltpu.VMEM((2, dp, t1, TILE, 2 * C), BF16),
        pltpu.VMEM((2, planes * t2, TILE, 2 * C), BF16),
        pltpu.VMEM((2, planes, t2, TILE, 2 * C), BF16),
        pltpu.VMEM((2, deep, t2, TILE, 2 * C), BF16),
        pltpu.VMEM((2, planes * t2, TILE, 2 * C), BF16),
        pltpu.SemaphoreType.DMA((4, 2)),
        pltpu.SemaphoreType.DMA((4, 2)),
        pltpu.SemaphoreType.DMA((5, 2, max(dp, planes, deep) - 1)),
        pltpu.SemaphoreType.DMA((5, 2, max(dp, planes, deep) - 1)),
    ]
    conv, gin, sums = pl.pallas_call(
        functools.partial(step_kernel, sizes),
        out_shape=(
            jax.ShapeDtypeStruct((C, n), BF16),
            jax.ShapeDtypeStruct((C, n), BF16),
            jax.ShapeDtypeStruct((2, dp, t1, TILE, 2 * C), BF16),
        ),
        in_specs=[pl.BlockSpec(memory_space=pltpu.VMEM)] * 5,
        out_specs=(pl.BlockSpec(memory_space=pltpu.VMEM),) * 3,
        scratch_shapes=scratch,
        compiler_params=pltpu.CompilerParams(
            collective_id=0, has_side_effects=True, vmem_limit_bytes=48 * 1024 * 1024
        ),
        name="step",
    )(feat, cot, rows, weight_one.reshape(K * C, C), weight_two.reshape(K * C, C))
    factor = float(dp * space * n) ** (-0.5)
    sums = sums.reshape(2, dp * t1 * TILE, 2, C)[:, : K * C // 2].reshape(2, K, C // 2, 2, C)
    grads = jnp.transpose(sums, (0, 1, 3, 2, 4)).reshape(2, K, C, C).astype(F32) * factor
    conv = conv.T.reshape(1, blocks, V * C)
    gin = gin.T.reshape(1, blocks, V * C)
    return conv, gin, grads[0], grads[1]


def solution(mesh):
    space, dp = mesh.shape["space"], mesh.shape["dp"]
    sizes = (space, dp, ZPAR * Y, space // (ZPAR * Y))
    wide = P("dp", "space", None)
    return jax.shard_map(
        functools.partial(per_device, sizes),
        mesh=mesh,
        in_specs=(wide, wide, wide, wide, P(), P()),
        out_specs=(wide, wide, P(), P()),
        check_vma=False,
    )
```

time: 253 us -> 64.5 us (0.25)
  the two profiles are of different devices: /device:TPU:32 before, /device:TPU:1 now
where the time goes in v1:
time: 64.5 us; the launch traced here: 64 us
  Pallas kernels  52.4 us (81%)
  local copies, waits for them, and re-layouts  9.22 us (14%)
  other arithmetic  1.69 us (3%)
  between operations  0.72 us (1%)
    pallas_call x1, Pallas kernels, per_device(): pl.pallas_call(functools.partial(step_kernel, sizes), out_shape=(jax.Shap...  52.4 us
    slice x3, local copies, waits for them, and re-layouts, per_device(): return (conv, gin, grads[0], grads[1])  2.19 us
    unnamed x4, local copies, waits for them, and re-layouts  2.02 us

profile of v1, /device:TPU:1, one launch (start us, length us, event | category | flops | bytes accessed | tf_op | source)
XLA Modules:
  0.0 64.0 jit_solution(14760623196475406136)
XLA Ops:
  0.6 0.7 %select_multiply_fusion = s32[4,27]{1,0:T(4,128)S(1)} fusion(s32[1,4,27]{2,1,0:T(4,128)} %param.7, s32[]{:T(128)S(6)} %axis_index.15), kind=kLoop, calls=%fused_computation.10 | loop fusion | flops 2808 | bytes 868 | tf_op jit(solution)/shard_map/mul | solution.py:331
  1.3 0.9 %reshape_squeeze.9 = bf16[256,64]{1,0:T(8,128)(2,1)S(1)} reshape(bf16[1,4,4096]{2,1,0:T(4,128)(2,1)} %param.6) | data formatting | bytes 65536 | tf_op jit(solution)/shard_map/reshape;squeeze | solution.py:333
  2.2 0.1 copy.14
  2.3 0.8 %reshape_squeeze.11 = s32[4,27,64]{2,1,0:T(8,128)S(1)} reshape(s32[1,4,1728]{2,1,0:T(4,128)} %param.8) | data formatting | bytes 55296 | tf_op jit(solution)/shard_map/reshape;squeeze | solution.py:330
  3.2 0.1 select_bitcast_fusion
  3.3 0.1 reshape.94.rows_ref
  3.4 0.9 %reshape_squeeze.10 = bf16[256,64]{1,0:T(8,128)(2,1)S(1)} reshape(bf16[1,4,4096]{2,1,0:T(4,128)(2,1)} %param.9) | data formatting | bytes 65536 | tf_op jit(solution)/shard_map/reshape;squeeze | solution.py:334
  4.3 0.1 copy.15
  4.4 0.0 copy-start
  4.4 1.0 %copy-done = bf16[27,64,64]{2,1,0:T(8,128)(2,1)S(1)} copy-done((bf16[27,64,64]{2,1,0:T(8,128)(2,1)S(1)}, bf16[27,64,64]{2,1,0:T(8,128)(2,1)}, u32[]{:S(2)}) %copy-start) | copy-done | bytes 221208
  5.4 0.0 copy-start.1
  5.4 1.0 %copy-done.1 = bf16[27,64,64]{2,1,0:T(8,128)(2,1)S(1)} copy-done((bf16[27,64,64]{2,1,0:T(8,128)(2,1)S(1)}, bf16[27,64,64]{2,1,0:T(8,128)(2,1)}, u32[]{:S(2)}) %copy-start.1) | copy-done | bytes 221208
  6.4 52.4 %step.1 = (bf16[64,256]{1,0:T(8,128)(2,1)S(1)}, bf16[64,256]{1,0:T(8,128)(2,1)S(1)}, bf16[2,8,7,16,128]{4,3,2,1,0:T(8,128)(2,1)S(1)}) custom-call(bf16[64,256]{1,0:T(8,128)(2,1)S(1)} %bitcast.35, bf16[64,256]{1,0:T(8,128)(2,1)S(1)} %bitcast.36, s32[27,1,256]{2,1,0:T(1,128)S(1)} %reshape.94.rows_ref, bf16[1728,64]{1,0:T(8,128)(2,1)S(1)} %bitcast.33, ...), custom_call_target="tpu_custom_call" | custom-call | tf_op jit(solution)/shard_map/step/pallas_call | solution.py:360
  58.8 0.1 copy.18
  58.9 0.7 %reshape.98 = bf16[1,4,4096]{2,1,0:T(4,128)(2,1)} reshape(bf16[256,64]{1,0:T(8,128)(2,1)S(1)} %copy.18) | data formatting | bytes 65536 | tf_op jit(solution)/shard_map/reshape | solution.py:379
  59.7 0.1 copy.17
  59.8 0.7 %reshape.97 = bf16[1,4,4096]{2,1,0:T(4,128)(2,1)} reshape(bf16[256,64]{1,0:T(8,128)(2,1)S(1)} %copy.17) | data formatting | bytes 65536 | tf_op jit(solution)/shard_map/reshape | solution.py:378
  60.5 0.4 reshape.99
  60.9 0.9 %convert_multiply_fusion = f32[2,864,2,64]{3,2,1,0:T(2,128)S(1)} fusion(bf16[2,896,2,64]{3,2,1,0:T(2,128)(2,1)S(1)} %reshape.99), kind=kLoop, calls=%fused_computation | loop fusion | flops 442368 | bytes 1327104 | tf_op jit(solution)/shard_map/mul | solution.py:377
  61.8 0.2 fusion.2
  62.0 1.0 %copy.20 = f32[1,27,2,32,64]{4,3,2,1,0:T(8,128)} copy(f32[1,27,2,32,64]{4,2,3,1,0:T(2,128)S(1)} %get-tuple-element.10) | data formatting | bytes 884736 | tf_op jit(solution)/shard_map/slice | solution.py:380
  63.0 1.0 %copy.19 = f32[1,27,2,32,64]{4,3,2,1,0:T(8,128)} copy(f32[1,27,2,32,64]{4,2,3,1,0:T(2,128)S(1)} %get-tuple-element.11) | data formatting | bytes 884736 | tf_op jit(solution)/shard_map/slice | solution.py:380
  (1 shorter events, 0.0 us)
Async XLA Ops:
  4.4 1.0 %copy-start = (bf16[27,64,64]{2,1,0:T(8,128)(2,1)S(1)}, bf16[27,64,64]{2,1,0:T(8,128)(2,1)}, u32[]{:S(2)}) copy-start(bf16[27,64,64]{2,1,0:T(8,128)(2,1)} %param.10) | copy-start | bytes 663556
  5.4 1.0 %copy-start.1 = (bf16[27,64,64]{2,1,0:T(8,128)(2,1)S(1)}, bf16[27,64,64]{2,1,0:T(8,128)(2,1)}, u32[]{:S(2)}) copy-start(bf16[27,64,64]{2,1,0:T(8,128)(2,1)} %param.11) | copy-start | bytes 663556

commit v2 on v1

v2 whole, which is shorter than its diff:
```python
import functools

import jax
import jax.numpy as jnp
from jax import lax
from jax.experimental import pallas as pl
from jax.experimental.pallas import tpu as pltpu
from jax.sharding import PartitionSpec as P

C = 64
V = 64
K = 27
HALO = 2
Y = 4
ZPAR = 2
CORES = 2
TILE = 16
TILES = K * C * C // (TILE * 2 * C)
MESH = pl.DeviceIdType.MESH
BF16 = jnp.bfloat16
F32 = jnp.float32


def mxu(a, b, dims=((1,), (0,))):
    return lax.dot_general(a, b, (dims, ((), ())), preferred_element_type=F32)


def step_kernel(
    sizes,
    feat_ref,
    cot_ref,
    rows_ref,
    w1_hbm,
    w2_hbm,
    conv_ref,
    gin_ref,
    sum1_ref,
    sum2_ref,
    hots,
    picked1,
    picked2,
    back,
    w1_ref,
    w2_ref,
    w1t,
    w2t,
    halo_in,
    halo_mid,
    rim_out,
    rim_in,
    hidden,
    parts,
    got1,
    mid,
    got2,
    got3,
    load_sem,
    halo_send,
    halo_recv,
    pair_send,
    pair_recv,
    group_send,
    group_recv,
    deep_send,
    deep_recv,
    relay,
):
    n_x, n_y, n_z = sizes
    deep = n_z // ZPAR
    space = n_y * n_z
    n = feat_ref.shape[1]
    half = n // 2
    s = lax.axis_index("space")
    d = lax.axis_index("dp")
    x, core = d // CORES, d % CORES
    z, y = s // n_y, s % n_y
    z_par, depth = z % ZPAR, z // ZPAR
    pad = TILES // CORES

    def at(dx=0, dy=0, dz=0, core=core):
        return (((z + dz) % n_z) * n_y + (y + dy) % n_y, ((x + dx) % n_x) * CORES + core)

    before = ((s + space - 1) % space, d)
    after = ((s + 1) % space, d)
    twin = at(core=1 - core)
    x_pair = [at(dx=1), at(dx=n_x - 1)]
    y_pair = [at(dy=1), at(dy=n_y - 1)]

    def z_pair(step):
        return [at(dz=step), at(dz=n_z - step)]

    other_z = (((z // ZPAR) * ZPAR + 1 - z_par) * n_y + y, d)

    def signal(sem, devices):
        for device in devices:
            pl.semaphore_signal(sem, inc=1, device_id=device, device_id_type=MESH)

    barrier = pltpu.get_barrier_semaphore()
    near = [before, after, twin] + x_pair + y_pair + z_pair(1)
    signal(barrier, near)

    z_steps = []
    while 2 ** len(z_steps) < n_z // 2:
        z_steps.append(2 ** len(z_steps))

    def relay_signal(i):
        if i == 0:
            signal(relay.at[0], x_pair)
        elif i <= 2:
            signal(relay.at[i], y_pair)
        else:
            signal(relay.at[i], [other_z])
        if i < len(z_steps):
            signal(relay.at[4 + i], z_pair(z_steps[i]))

    def relay_wait(i):
        pl.semaphore_wait(relay.at[i], 2 if i <= 2 else 1)
        if i < len(z_steps) - 1:
            pl.semaphore_wait(relay.at[4 + i], 2)

    def relay_end():
        pl.semaphore_wait(relay.at[4 + len(z_steps) - 1], 2)

    def remote(src, dst, send, recv, target):
        return pltpu.make_async_remote_copy(
            src_ref=src, dst_ref=dst, send_sem=send, recv_sem=recv, device_id=target, device_id_type=MESH
        )

    loads = [
        pltpu.make_async_copy(w2_hbm, w2_ref, load_sem.at[0]),
        pltpu.make_async_copy(w1_hbm, w1_ref, load_sem.at[1]),
    ]
    for load in loads:
        load.start()

    spot = lax.broadcasted_iota(jnp.int32, (n, n), 0).astype(F32).astype(BF16)
    one_hot = jnp.ones((n, n), BF16)
    no_hot = jnp.zeros((n, n), BF16)

    def build(k, carry):
        row = rows_ref[k].astype(F32)
        lanes = pl.ds(pl.multiple_of(k * n, n), n)
        hots[0:n, lanes] = jnp.where(spot == row.astype(BF16), one_hot, no_hot)
        hots[n : 2 * n, lanes] = jnp.where(spot == (row - n).astype(BF16), one_hot, no_hot)
        return carry

    lax.fori_loop(0, K, build, 0)

    group_of = 9

    def spread(w_ref, grad):
        for g in range(0, K, group_of):
            out = mxu(w_ref[g * C : (g + group_of) * C, :], grad).astype(BF16)
            for k in range(group_of):
                back[:, (g + k) * n : (g + k + 1) * n] = out[k * C : (k + 1) * C, :]

    def scattered(lo, hi):
        def some(g, total):
            lanes = pl.ds(pl.multiple_of(g * group_of * n, group_of * n), group_of * n)
            return total + mxu(back[:, lanes], hots[lo:hi, lanes], ((1,), (1,)))

        return lax.fori_loop(0, K // group_of, some, jnp.zeros((C, hi - lo), F32))

    def pick_own(table, picked):
        def one(g, carry):
            for i in range(group_of):
                k = g * group_of + i
                lanes = pl.ds(pl.multiple_of(k * n, n), n)
                picked[k] = mxu(table, hots[0:n, lanes]).astype(BF16)
            return carry

        lax.fori_loop(0, K // group_of, one, 0)

    def pick_halo(table, picked):
        def one(g, carry):
            for i in range(group_of):
                k = g * group_of + i
                lanes = pl.ds(pl.multiple_of(k * n, n), n)
                more = mxu(table, hots[n : 2 * n, lanes])
                picked[k] = (picked[k].astype(F32) + more).astype(BF16)
            return carry

        lax.fori_loop(0, K // group_of, one, 0)

    def convolved(wt, picked):
        return mxu(wt[...], picked[...].reshape(K * C, n))

    def weight_parts(which, picked, grad):
        zero = jnp.zeros((C, n), BF16)
        pair = jnp.concatenate(
            [jnp.concatenate([grad, zero], axis=1), jnp.concatenate([zero, grad], axis=1)], axis=0
        )
        for g in range(0, K, group_of):
            both = jnp.concatenate(
                [picked[g : g + group_of, 0 : C // 2, :], picked[g : g + group_of, C // 2 : C, :]], axis=2
            ).reshape(group_of * C // 2, 2 * n)
            out = mxu(both, pair, ((1,), (1,))).astype(BF16)
            tiles = group_of * C // 2 // TILE
            out = out.reshape(tiles, TILE, 2 * C)
            first = g * C // 2 // TILE
            cut = min(max(pad - first, 0), tiles)
            if cut > 0:
                parts[which, 0, first : first + cut] = out[:cut]
            if cut < tiles:
                parts[which, 1, first + cut - pad : first + tiles - pad] = out[cut:]

    def to_neighbours(slot, low, high, into):
        copies = [
            remote(low, into.at[1], halo_send.at[slot, 0], halo_recv.at[slot, 1], before),
            remote(high, into.at[0], halo_send.at[slot, 1], halo_recv.at[slot, 0], after),
        ]
        for copy in copies:
            copy.start()
        return copies

    def arrive(copies):
        for copy in copies:
            copy.wait_recv()

    offsets = [
        (dx, dy, dz) for dx in range(n_x) for dy in range(n_y) for dz in range(ZPAR) if (dx, dy, dz) != (0, 0, 0)
    ]
    offsets.sort(key=lambda o: -(min(o[0], n_x - o[0]) + min(o[1], n_y - o[1]) + o[2]))

    def member(x, y, z):
        return (z * n_y + y) * n_x + x

    me = member(x, y, z_par)

    def to_twin(stage, which, src, dst):
        copy = remote(src, dst, pair_send.at[stage, which], pair_recv.at[stage, which], twin)
        copy.start()
        return [copy]

    def to_members(stage, which, src_of, dst):
        copies = []
        for i, (dx, dy, dz) in enumerate(offsets):
            xx, yy, zz = (x + dx) % n_x, (y + dy) % n_y, (z_par + dz) % ZPAR
            target = (((z // ZPAR) * ZPAR + zz) * n_y + yy, xx * CORES + core)
            copy = remote(
                src_of(member(xx, yy, zz)), dst, group_send.at[stage, which, i], group_recv.at[stage, which, i], target
            )
            copy.start()
            copies.append(copy)
        return copies

    def to_depths(which, src, dst):
        copies = []
        for j in [j for i in range(deep // 2, 0, -1) for j in sorted({i, deep - i})]:
            target = at(dz=j * ZPAR)
            copy = remote(src, dst, deep_send.at[which, j - 1], deep_recv.at[which, j - 1], target)
            copy.start()
            copies.append(copy)
        return copies

    feat = feat_ref[...]
    cot = cot_ref[...]
    for which in range(2):
        mid[which, pad] = jnp.zeros((TILE, 2 * C), BF16)
    loads[0].wait()
    spread(w2_ref, cot)
    pl.semaphore_wait(barrier, len(near))
    relay_signal(0)
    feat_copies = to_neighbours(0, feat_ref.at[:, 0:half], feat_ref.at[:, half:n], halo_in)
    rim = scattered(n, 2 * n).astype(BF16)
    for i in range(2):
        rim_out[0, i] = rim[:, i * half : (i + 1) * half]
    rim_copies = to_neighbours(1, rim_out.at[0, 0], rim_out.at[0, 1], rim_in.at[0])
    sent = feat_copies + rim_copies
    relay_wait(0)
    relay_signal(1)

    pick_own(feat, picked1)
    relay_wait(1)
    relay_signal(2)
    loads[1].wait()
    w1t[...] = w1_ref[...].T
    w2t[...] = w2_ref[...].T

    arrive(feat_copies)
    pick_halo(jnp.concatenate([halo_in[0], halo_in[1]], axis=1), picked1)
    pre = convolved(w1t, picked1)
    sig = 1.0 / (1.0 + jnp.exp(-pre))
    hid = (pre * sig).astype(BF16)
    hidden[...] = hid
    hid_copies = to_neighbours(2, hidden.at[:, 0:half], hidden.at[:, half:n], halo_mid)
    sent += hid_copies
    relay_wait(2)
    relay_signal(3)

    grad_hidden = scattered(0, n)
    arrive(rim_copies)
    rims = jnp.concatenate([rim_in[0, 0], rim_in[0, 1]], axis=1).astype(F32)
    grad_pre = ((grad_hidden + rims) * (sig * (1.0 + pre * (1.0 - sig)))).astype(BF16)
    weight_parts(0, picked1, grad_pre)

    def reduce_pair(which):
        return to_twin(0, which, parts.at[which, 1 - core], got1.at[which])

    def scatter_reduce(which, copies):
        arrive(copies)
        mid[which, 0:pad] = (parts[which, core].astype(F32) + got1[which].astype(F32)).astype(BF16)
        got2[which, me] = mid[which, jnp.minimum(me, pad)]
        return to_members(0, which, lambda other: mid.at[which, jnp.minimum(other, pad)], got2.at[which, me])

    def added(ref, which, count):
        totals = [ref[which, i].astype(F32) for i in range(count)]
        while len(totals) > 1:
            totals = [a + b for a, b in zip(totals[::2], totals[1::2])]
        return totals[0].astype(BF16)

    def reduce_deep(which, copies):
        arrive(copies)
        got3[which, depth] = added(got2, which, len(offsets) + 1)
        mine = got3.at[which, depth]
        return to_depths(which, mine, mine)

    def gather_members(which, copies, out):
        arrive(copies)
        out[core, me] = added(got3, which, deep)
        mine = out.at[core, me]
        return to_members(1, which, lambda other: mine, mine)

    def gather_pair(which, copies, out):
        arrive(copies)
        mine = out.at[core, 0:pad]
        return to_twin(1, which, mine, mine)

    one = reduce_pair(0)
    sent += one

    pick_own(hid, picked2)
    relay_wait(3)
    one = scatter_reduce(0, one)
    sent += one
    arrive(hid_copies)
    pick_halo(jnp.concatenate([halo_mid[0], halo_mid[1]], axis=1), picked2)
    weight_parts(1, picked2, cot)
    two = reduce_pair(1)
    sent += two

    spread(w1_ref, grad_pre)
    rim = scattered(n, 2 * n).astype(BF16)
    for i in range(2):
        rim_out[1, i] = rim[:, i * half : (i + 1) * half]
    last_copies = to_neighbours(3, rim_out.at[1, 0], rim_out.at[1, 1], rim_in.at[1])
    sent += last_copies
    two = scatter_reduce(1, two)
    sent += two
    relay_end()
    one = reduce_deep(0, one)
    sent += one

    conv_ref[...] = convolved(w2t, picked2).astype(BF16)
    grad_in = scattered(0, n)
    arrive(last_copies)
    rims = jnp.concatenate([rim_in[1, 0], rim_in[1, 1]], axis=1).astype(F32)
    gin_ref[...] = (grad_in + rims).astype(BF16)

    two = reduce_deep(1, two)
    sent += two
    one = gather_members(0, one, sum1_ref)
    sent += one
    two = gather_members(1, two, sum2_ref)
    sent += two
    one = gather_pair(0, one, sum1_ref)
    sent += one
    two = gather_pair(1, two, sum2_ref)
    sent += two
    arrive(one)
    arrive(two)
    for copy in sent:
        copy.wait_send()


def per_device(sizes, features, sources, voxels, cotangent, weight_one, weight_two):
    n_x, n_y, n_z = sizes
    members = n_x * n_y * ZPAR
    deep = n_z // ZPAR
    blocks = features.shape[1]
    n = blocks * V
    half = n // 2
    me = lax.axis_index("space")
    source_ids = sources[0]
    owner = source_ids // blocks
    place = source_ids % blocks
    slot = jnp.where(owner == me, place, jnp.where(owner < me, place + HALO, blocks + HALO + place))
    vox = voxels[0].reshape(blocks, K, V)
    rows = jnp.where(vox == V, -1, slot[:, :, None] * V + vox)
    rows = jnp.transpose(rows, (1, 0, 2)).reshape(K, 1, n)
    feat = features[0].reshape(n, C).T
    cot = cotangent[0].reshape(n, C).T
    pad = TILES // CORES
    scratch = [
        pltpu.VMEM((2 * n, K * n), BF16),
        pltpu.VMEM((K, C, n), BF16),
        pltpu.VMEM((K, C, n), BF16),
        pltpu.VMEM((C, K * n), BF16),
        pltpu.VMEM((K * C, C), BF16),
        pltpu.VMEM((K * C, C), BF16),
        pltpu.VMEM((C, K * C), BF16),
        pltpu.VMEM((C, K * C), BF16),
        pltpu.VMEM((2, C, half), BF16),
        pltpu.VMEM((2, C, half), BF16),
        pltpu.VMEM((2, 2, C, half), BF16),
        pltpu.VMEM((2, 2, C, half), BF16),
        pltpu.VMEM((C, n), BF16),
        pltpu.VMEM((2, CORES, pad, TILE, 2 * C), BF16),
        pltpu.VMEM((2, pad, TILE, 2 * C), BF16),
        pltpu.VMEM((2, pad + 1, TILE, 2 * C), BF16),
        pltpu.VMEM((2, members, TILE, 2 * C), BF16),
        pltpu.VMEM((2, deep, TILE, 2 * C), BF16),
        pltpu.SemaphoreType.DMA((2,)),
        pltpu.SemaphoreType.DMA((4, 2)),
        pltpu.SemaphoreType.DMA((4, 2)),
        pltpu.SemaphoreType.DMA((2, 2)),
        pltpu.SemaphoreType.DMA((2, 2)),
        pltpu.SemaphoreType.DMA((2, 2, members - 1)),
        pltpu.SemaphoreType.DMA((2, 2, members - 1)),
        pltpu.SemaphoreType.DMA((2, deep - 1)),
        pltpu.SemaphoreType.DMA((2, deep - 1)),
        pltpu.SemaphoreType.REGULAR((8,)),
    ]
    total = jax.ShapeDtypeStruct((CORES, members, TILE, 2 * C), BF16)
    vmem = pl.BlockSpec(memory_space=pltpu.VMEM)
    hbm = pl.BlockSpec(memory_space=pl.ANY)
    conv, gin, sum1, sum2 = pl.pallas_call(
        functools.partial(step_kernel, sizes),
        out_shape=(jax.ShapeDtypeStruct((C, n), BF16), jax.ShapeDtypeStruct((C, n), BF16), total, total),
        in_specs=[vmem, vmem, vmem, hbm, hbm],
        out_specs=(vmem,) * 4,
        scratch_shapes=scratch,
        compiler_params=pltpu.CompilerParams(
            collective_id=0, has_side_effects=True, vmem_limit_bytes=48 * 1024 * 1024
        ),
        name="step",
    )(feat, cot, rows, weight_one.reshape(K * C, C), weight_two.reshape(K * C, C))
    factor = float(n_x * CORES * n_y * n_z * n) ** (-0.5)

    def whole(tiles):
        pairs = tiles[:, :pad].reshape(K, C // 2, 2, C)
        return jnp.transpose(pairs, (0, 2, 1, 3)).reshape(K, C, C).astype(F32) * factor

    conv = conv.T.reshape(1, blocks, V * C)
    gin = gin.T.reshape(1, blocks, V * C)
    return conv, gin, whole(sum1), whole(sum2)


def solution(mesh):
    space, dp = mesh.shape["space"], mesh.shape["dp"]
    sizes = (dp // CORES, Y, space // Y)
    wide = P("dp", "space", None)
    return jax.shard_map(
        functools.partial(per_device, sizes),
        mesh=mesh,
        in_specs=(wide, wide, wide, wide, P(), P()),
        out_specs=(wide, wide, P(), P()),
        check_vma=False,
    )
```

time: 64.5 us -> 60.1 us (0.932)
  Pallas kernels: 52.4 us -> 49.5 us
  other arithmetic: 1.69 us -> 0.91 us
    mul x0 -> x4, local copies, waits for them, and re-layouts: none -> 3.08 us  [whole(): jnp.transpose(pairs, (0, 2, 1, 3)).reshape(K, C, C).astype(F32) * factor]
    pallas_call x1, Pallas kernels: 52.4 us -> 49.5 us  [per_device(): pl.pallas_call(functools.partial(step_kernel, sizes), out_shape=(jax.Shap...]
    slice x3 -> x0, local copies, waits for them, and re-layouts: 2.19 us -> none  [per_device(): return (conv, gin, grads[0], grads[1])]
    mul x1, other arithmetic: 0.91 us -> 0.08 us  [whole(): jnp.transpose(pairs, (0, 2, 1, 3)).reshape(K, C, C).astype(F32) * factor]
    another operation x2, local copies, waits for them, and re-layouts: 0.97 us -> 0.21 us  [per_device(): cot = cotangent[0].reshape(n, C).T]
    unnamed x4 -> x6, local copies, waits for them, and re-layouts: 2.02 us -> 1.66 us
where the time goes in v2:
time: 60.1 us; the launch traced here: 59.8 us
  Pallas kernels  49.5 us (82%)
  local copies, waits for them, and re-layouts  8.61 us (14%)
  other arithmetic  0.91 us (2%)
  between operations  0.75 us (1%)
    pallas_call x1, Pallas kernels, per_device(): pl.pallas_call(functools.partial(step_kernel, sizes), out_shape=(jax.Shap...  49.5 us
    mul x4, local copies, waits for them, and re-layouts, whole(): jnp.transpose(pairs, (0, 2, 1, 3)).reshape(K, C, C).astype(F32) * factor  3.08 us
    unnamed x6, local copies, waits for them, and re-layouts  1.66 us

profile of v2, /device:TPU:1, one launch (start us, length us, event | category | flops | bytes accessed | tf_op | source)
XLA Modules:
  0.0 59.8 jit_solution(12314407959297384206)
XLA Ops:
  0.6 0.0 copy-start
  0.6 0.7 %select_multiply_fusion = s32[4,27]{1,0:T(4,128)S(1)} fusion(s32[1,4,27]{2,1,0:T(4,128)} %param.7, s32[]{:T(128)S(6)} %axis_index.15), kind=kLoop, calls=%fused_computation.11 | loop fusion | flops 2808 | bytes 868 | tf_op jit(solution)/shard_map/mul | solution.py:389
  1.4 0.9 %reshape_squeeze.9 = bf16[256,64]{1,0:T(8,128)(2,1)S(1)} reshape(bf16[1,4,4096]{2,1,0:T(4,128)(2,1)} %param.6) | data formatting | bytes 65536 | tf_op jit(solution)/shard_map/reshape;squeeze | solution.py:391
  2.3 0.1 copy.15
  2.4 0.8 %reshape_squeeze.11 = s32[4,27,64]{2,1,0:T(8,128)S(1)} reshape(s32[1,4,1728]{2,1,0:T(4,128)} %param.8) | data formatting | bytes 55296 | tf_op jit(solution)/shard_map/reshape;squeeze | solution.py:388
  3.2 0.1 select_bitcast_fusion
  3.3 0.0 copy-start.2
  3.4 0.1 reshape.95.rows_ref
  3.5 0.6 %copy-done.2 = bf16[1,4,4096]{2,1,0:T(4,128)(2,1)S(1)} copy-done((bf16[1,4,4096]{2,1,0:T(4,128)(2,1)S(1)}, bf16[1,4,4096]{2,1,0:T(4,128)(2,1)}, u32[]{:S(2)}) %copy-start.2) | copy-done | bytes 32792
  4.1 0.1 reshape_squeeze.10
  4.2 0.1 copy.16
  4.3 0.0 copy-done
  4.3 0.0 copy-start.1
  4.4 1.0 %copy-done.1 = bf16[27,64,64]{2,1,0:T(8,128)(2,1)S(1)} copy-done((bf16[27,64,64]{2,1,0:T(8,128)(2,1)S(1)}, bf16[27,64,64]{2,1,0:T(8,128)(2,1)}, u32[]{:S(2)}) %copy-start.1) | copy-done | bytes 221208
  5.4 49.5 %step.1 = (bf16[64,256]{1,0:T(8,128)(2,1)S(1)}, bf16[64,256]{1,0:T(8,128)(2,1)S(1)}, bf16[2,32,16,128]{3,2,1,0:T(8,128)(2,1)S(1)}, bf16[2,32,16,128]{3,2,1,0:T(8,128)(2,1)S(1)}) custom-call(bf16[64,256]{1,0:T(8,128)(2,1)S(1)} %bitcast.36, bf16[64,256]{1,0:T(8,128)(2,1)S(1)} %bitcast.37, s32[27,1,256]{2,1,0:T(1,128)S(1)} %reshape.95.rows_ref, ...), custom_call_target="tpu_custom_call" | custom-call | tf_op jit(solution)/shard_map/step/pallas_call | solution.py:427
  54.9 0.1 copy.19
  55.0 0.7 %reshape.99 = bf16[1,4,4096]{2,1,0:T(4,128)(2,1)} reshape(bf16[256,64]{1,0:T(8,128)(2,1)S(1)} %copy.19) | data formatting | bytes 65536 | tf_op jit(solution)/shard_map/reshape | solution.py:445
  55.7 0.1 copy.18
  55.8 0.7 %reshape.98 = bf16[1,4,4096]{2,1,0:T(4,128)(2,1)} reshape(bf16[256,64]{1,0:T(8,128)(2,1)S(1)} %copy.18) | data formatting | bytes 65536 | tf_op jit(solution)/shard_map/reshape | solution.py:444
  56.6 0.1 convert_multiply_fusion
  56.7 0.5 mul.42
  57.2 1.0 %copy.21 = f32[27,2,32,64]{3,2,1,0:T(8,128)} copy(f32[27,2,32,64]{3,1,2,0:T(2,128)S(1)} %bitcast.40) | data formatting | bytes 884736 | tf_op jit(solution)/shard_map/mul | solution.py:442
  58.2 0.5 mul.38
  58.8 1.0 %copy.20 = f32[27,2,32,64]{3,2,1,0:T(8,128)} copy(f32[27,2,32,64]{3,1,2,0:T(2,128)S(1)} %bitcast.41) | data formatting | bytes 884736 | tf_op jit(solution)/shard_map/mul | solution.py:442
  (1 shorter events, 0.0 us)
Async XLA Ops:
  0.6 3.7 %copy-start = (bf16[27,64,64]{2,1,0:T(8,128)(2,1)S(1)}, bf16[27,64,64]{2,1,0:T(8,128)(2,1)}, u32[]{:S(2)}) copy-start(bf16[27,64,64]{2,1,0:T(8,128)(2,1)} %param.10) | copy-start | bytes 663556
  3.3 0.8 %copy-start.2 = (bf16[1,4,4096]{2,1,0:T(4,128)(2,1)S(1)}, bf16[1,4,4096]{2,1,0:T(4,128)(2,1)}, u32[]{:S(2)}) copy-start(bf16[1,4,4096]{2,1,0:T(4,128)(2,1)} %param.9) | copy-start | bytes 98308
  4.3 1.0 %copy-start.1 = (bf16[27,64,64]{2,1,0:T(8,128)(2,1)S(1)}, bf16[27,64,64]{2,1,0:T(8,128)(2,1)}, u32[]{:S(2)}) copy-start(bf16[27,64,64]{2,1,0:T(8,128)(2,1)} %param.11) | copy-start | bytes 663556

commit v3 on v2

v3 whole, which is shorter than its diff:
```python
import functools

import jax
import jax.numpy as jnp
from jax import lax
from jax.experimental import pallas as pl
from jax.experimental.pallas import tpu as pltpu
from jax.sharding import PartitionSpec as P

C = 64
V = 64
K = 27
HALO = 2
Y = 4
ZPAR = 2
CORES = 2
TILE = 16
TILES = K * C * C // (TILE * 2 * C)
MESH = pl.DeviceIdType.MESH
BF16 = jnp.bfloat16
F32 = jnp.float32


def mxu(a, b, dims=((1,), (0,))):
    return lax.dot_general(a, b, (dims, ((), ())), preferred_element_type=F32)


def step_kernel(
    sizes,
    x_hbm,
    ct_hbm,
    src_hbm,
    vox_hbm,
    w1_hbm,
    w2_hbm,
    conv_ref,
    gin_ref,
    grad1_ref,
    grad2_ref,
    x_ref,
    ct_ref,
    src_ref,
    vox_ref,
    w1_ref,
    w2_ref,
    slots,
    pair_rows,
    wide_rows,
    turn,
    flat,
    table1,
    table2,
    feat_ref,
    picked1,
    picked2,
    back,
    w1t,
    w2t,
    halo_in,
    halo_mid,
    rim_out,
    rim_in,
    hidden,
    parts,
    got1,
    mid,
    got2,
    got3,
    sums,
    load_sem,
    halo_send,
    halo_recv,
    pair_send,
    pair_recv,
    group_send,
    group_recv,
    deep_send,
    deep_recv,
    relay,
):
    n_x, n_y, n_z = sizes
    deep = n_z // ZPAR
    space = n_y * n_z
    blocks = x_ref.shape[0]
    n = feat_ref.shape[1]
    half = n // 2
    s = lax.axis_index("space")
    d = lax.axis_index("dp")
    x, core = d // CORES, d % CORES
    z, y = s // n_y, s % n_y
    z_par, depth = z % ZPAR, z // ZPAR
    pad = TILES // CORES
    per = sums.shape[2] // (n_x * n_y * ZPAR)

    def at(dx=0, dy=0, dz=0, core=core):
        return (((z + dz) % n_z) * n_y + (y + dy) % n_y, ((x + dx) % n_x) * CORES + core)

    before = ((s + space - 1) % space, d)
    after = ((s + 1) % space, d)
    twin = at(core=1 - core)
    x_pair = [at(dx=1), at(dx=n_x - 1)]
    y_pair = [at(dy=1), at(dy=n_y - 1)]

    def z_pair(step):
        return [at(dz=step), at(dz=n_z - step)]

    other_z = (((z // ZPAR) * ZPAR + 1 - z_par) * n_y + y, d)

    def signal(sem, devices):
        for device in devices:
            pl.semaphore_signal(sem, inc=1, device_id=device, device_id_type=MESH)

    barrier = pltpu.get_barrier_semaphore()
    near = [before, after, twin] + x_pair + y_pair + z_pair(1)
    signal(barrier, near)

    z_steps = []
    while 2 ** len(z_steps) < n_z // 2:
        z_steps.append(2 ** len(z_steps))

    def relay_signal(i):
        if i == 0:
            signal(relay.at[0], x_pair)
        elif i <= 2:
            signal(relay.at[i], y_pair)
        else:
            signal(relay.at[i], [other_z])
        if i < len(z_steps):
            signal(relay.at[4 + i], z_pair(z_steps[i]))

    def relay_wait(i):
        pl.semaphore_wait(relay.at[i], 2 if i <= 2 else 1)
        if i < len(z_steps) - 1:
            pl.semaphore_wait(relay.at[4 + i], 2)

    def relay_end():
        pl.semaphore_wait(relay.at[4 + len(z_steps) - 1], 2)

    def remote(src, dst, send, recv, target):
        return pltpu.make_async_remote_copy(
            src_ref=src, dst_ref=dst, send_sem=send, recv_sem=recv, device_id=target, device_id_type=MESH
        )

    loads = {}
    for i, (name, src, dst) in enumerate(
        (
            ("vox", vox_hbm, vox_ref),
            ("src", src_hbm, src_ref),
            ("x", x_hbm, x_ref),
            ("ct", ct_hbm, ct_ref),
            ("w2", w2_hbm, w2_ref),
            ("w1", w1_hbm, w1_ref),
        )
    ):
        loads[name] = pltpu.make_async_copy(src, dst, load_sem.at[i])
        loads[name].start()

    def iota(shape, dim):
        return lax.broadcasted_iota(jnp.int32, shape, dim)

    pairs = V // 2
    old = iota((n, n), 0)
    parity, rest = old // (n // 2), old % (n // 2)
    order = jnp.where(rest // pairs * V + rest % pairs * 2 + parity == iota((n, n), 1), 1.0, 0.0).astype(BF16)

    def to_channels(ref):
        wide = ref[...].astype(F32)
        for j in range(pairs):
            turn[j * blocks : (j + 1) * blocks, :] = wide[:, j * 2 * C : (j + 1) * 2 * C]
        rows = jnp.concatenate([turn[pl.ds(b, pairs, stride=blocks), :] for b in range(blocks)], axis=0)
        lanes = rows.T
        both = jnp.concatenate([lanes[:C], lanes[C:]], axis=1).astype(BF16)
        return mxu(both, order).astype(BF16)

    def from_channels(value, out_ref):
        both = mxu(value, order, ((1,), (1,)))
        rows = jnp.concatenate([both[:, : n // 2], both[:, n // 2 :]], axis=0).T
        turn[...] = rows
        for j in range(pairs):
            flat[:, j * 2 * C : (j + 1) * 2 * C] = turn[pl.ds(j, blocks, stride=pairs), :]
        out_ref[...] = flat[...].astype(BF16)

    low_row = iota((1, 2 * V), 1) < V
    shift = blocks.bit_length() - 1

    def make_rows():
        for k in range(K):
            for b in range(blocks):
                source = src_ref[b, k]
                owner, place = source >> shift, source & (blocks - 1)
                slots[k * blocks + b] = jnp.where(
                    owner == s, place, jnp.where(owner < s, place + HALO, blocks + HALO + place)
                )
            start = k // 2 * 2 * V
            if start + 2 * V <= K * V:
                here = vox_ref[:, start : start + 2 * V]
            else:
                here = jnp.concatenate([vox_ref[:, start : start + V]] * 2, axis=1)
            there = pltpu.roll(here, V, 1)
            first, second = (here, there) if k % 2 == 0 else (there, here)
            for p in range(blocks // 2):
                row = jnp.where(low_row, first[2 * p : 2 * p + 1], second[2 * p + 1 : 2 * p + 2])
                none = row >= V
                base = jnp.where(low_row, slots[k * blocks + 2 * p] * V, slots[k * blocks + 2 * p + 1] * V)
                lanes = slice(p * 2 * V, (p + 1) * 2 * V)
                pair_rows[k, :, lanes] = jnp.where(none, -1, row + jnp.where(low_row, 0, V)).astype(F32)
                wide_rows[k, :, lanes] = jnp.where(none, -1, row + base).astype(F32)

    group_of = 9
    spot = iota((n, n), 0).astype(F32).astype(BF16)
    spot_pair = iota((2 * V, 2 * V), 0).astype(F32).astype(BF16)

    def hot(where, row):
        return jnp.where(where == row.astype(BF16), jnp.ones_like(where), jnp.zeros_like(where))

    def spread(w_ref, grad):
        for g in range(0, K, group_of):
            out = mxu(w_ref[g * C : (g + group_of) * C, :], grad).astype(BF16)
            back[g : g + group_of] = out.reshape(group_of, C, n)

    def scattered(lo):
        def some(g, total):
            for i in range(group_of):
                k = g * group_of + i
                total = total + mxu(back[k], hot(spot, wide_rows[k] - lo), ((1,), (1,)))
            return total

        return lax.fori_loop(0, K // group_of, some, jnp.zeros((C, n), F32))

    low16 = iota((C, 2 * V), 1).astype(F32).astype(BF16) < V
    low32 = iota((C, 2 * V), 1) < V

    def fill(table, value, first):
        value = value.astype(F32)
        turned = pltpu.roll(value, V, 1)
        table[first] = jnp.where(low32, value, turned).astype(BF16)
        table[first + 1] = jnp.where(low32, turned, value).astype(BF16)

    def fill_own(table, value):
        for p in range(blocks // 2):
            fill(table, value[:, p * 2 * V : (p + 1) * 2 * V], 2 * p)

    def fill_halo(table, ref):
        for i in range(2):
            fill(table, ref[i], blocks + 2 * i)

    def pick(table, picked):
        def one(g, carry):
            for i in range(group_of):
                k = g * group_of + i
                for p in range(blocks // 2):
                    lanes = slice(p * 2 * V, (p + 1) * 2 * V)
                    both = jnp.where(
                        low16, table[slots[k * blocks + 2 * p]], table[slots[k * blocks + 2 * p + 1]]
                    )
                    picked[k, :, lanes] = mxu(both, hot(spot_pair, pair_rows[k, :, lanes])).astype(BF16)
            return carry

        lax.fori_loop(0, K // group_of, one, 0)

    def convolved(wt, picked):
        return mxu(wt[...], picked[...].reshape(K * C, n))

    def weight_parts(which, picked, grad):
        zero = jnp.zeros((C, n), BF16)
        pair = jnp.concatenate(
            [jnp.concatenate([grad, zero], axis=1), jnp.concatenate([zero, grad], axis=1)], axis=0
        )
        for g in range(0, K, group_of):
            both = jnp.concatenate(
                [picked[g : g + group_of, 0 : C // 2, :], picked[g : g + group_of, C // 2 : C, :]], axis=2
            ).reshape(group_of * C // 2, 2 * n)
            out = mxu(both, pair, ((1,), (1,))).astype(BF16)
            tiles = group_of * C // 2 // TILE
            out = out.reshape(tiles, TILE, 2 * C)
            first = g * C // 2 // TILE
            cut = min(max(pad - first, 0), tiles)
            if cut > 0:
                parts[which, 0, first : first + cut] = out[:cut]
            if cut < tiles:
                parts[which, 1, first + cut - pad : first + tiles - pad] = out[cut:]

    def to_neighbours(slot, low, high, into):
        copies = [
            remote(low, into.at[1], halo_send.at[slot, 0], halo_recv.at[slot, 1], before),
            remote(high, into.at[0], halo_send.at[slot, 1], halo_recv.at[slot, 0], after),
        ]
        for copy in copies:
            copy.start()
        return copies

    def arrive(copies):
        for copy in copies:
            copy.wait_recv()

    offsets = [
        (dx, dy, dz) for dx in range(n_x) for dy in range(n_y) for dz in range(ZPAR) if (dx, dy, dz) != (0, 0, 0)
    ]
    offsets.sort(key=lambda o: -(min(o[0], n_x - o[0]) + min(o[1], n_y - o[1]) + o[2]))

    def member(x, y, z):
        return (z * n_y + y) * n_x + x

    me = member(x, y, z_par)

    def to_twin(stage, which, src, dst):
        copy = remote(src, dst, pair_send.at[stage, which], pair_recv.at[stage, which], twin)
        copy.start()
        return [copy]

    def to_members(stage, which, src_of, dst):
        copies = []
        for i, (dx, dy, dz) in enumerate(offsets):
            xx, yy, zz = (x + dx) % n_x, (y + dy) % n_y, (z_par + dz) % ZPAR
            target = (((z // ZPAR) * ZPAR + zz) * n_y + yy, xx * CORES + core)
            copy = remote(
                src_of(member(xx, yy, zz)), dst, group_send.at[stage, which, i], group_recv.at[stage, which, i], target
            )
            copy.start()
            copies.append(copy)
        return copies

    def to_depths(which, src, dst):
        copies = []
        for j in [j for i in range(deep // 2, 0, -1) for j in sorted({i, deep - i})]:
            target = at(dz=j * ZPAR)
            copy = remote(src, dst, deep_send.at[which, j - 1], deep_recv.at[which, j - 1], target)
            copy.start()
            copies.append(copy)
        return copies

    for which in range(2):
        mid[which, pad:] = jnp.zeros((mid.shape[1] - pad, TILE, 2 * C), BF16)
    loads["x"].wait()
    feat = to_channels(x_ref)
    feat_ref[...] = feat
    pl.semaphore_wait(barrier, len(near))
    feat_copies = to_neighbours(0, feat_ref.at[:, 0:half], feat_ref.at[:, half:n], halo_in)
    relay_signal(0)
    sent = list(feat_copies)

    loads["vox"].wait()
    loads["src"].wait()
    make_rows()
    loads["ct"].wait()
    cot = to_channels(ct_ref)
    loads["w2"].wait()
    spread(w2_ref, cot)
    rim = scattered(n).astype(BF16)
    for i in range(2):
        rim_out[0, i] = rim[:, i * half : (i + 1) * half]
    rim_copies = to_neighbours(1, rim_out.at[0, 0], rim_out.at[0, 1], rim_in.at[0])
    sent += rim_copies
    relay_wait(0)
    relay_signal(1)
    loads["w1"].wait()
    w1t[...] = w1_ref[...].T
    fill_own(table1, feat)

    arrive(feat_copies)
    fill_halo(table1, halo_in)
    pick(table1, picked1)
    pre = convolved(w1t, picked1)
    sig = 1.0 / (1.0 + jnp.exp(-pre))
    hid = (pre * sig).astype(BF16)
    hidden[...] = hid
    hid_copies = to_neighbours(2, hidden.at[:, 0:half], hidden.at[:, half:n], halo_mid)
    sent += hid_copies
    relay_wait(1)
    relay_signal(2)

    grad_hidden = scattered(0)
    arrive(rim_copies)
    rims = jnp.concatenate([rim_in[0, 0], rim_in[0, 1]], axis=1).astype(F32)
    grad_pre = ((grad_hidden + rims) * (sig * (1.0 + pre * (1.0 - sig)))).astype(BF16)
    weight_parts(0, picked1, grad_pre)

    def mine_of(which):
        return sums.at[which, core, pl.ds(me * per, per)]

    def reduce_pair(which):
        return to_twin(0, which, parts.at[which, 1 - core], got1.at[which])

    def scatter_reduce(which, copies):
        arrive(copies)
        mid[which, 0:pad] = (parts[which, core].astype(F32) + got1[which].astype(F32)).astype(BF16)
        got2[which, me] = mid[which, pl.ds(me * per, per)]
        return to_members(0, which, lambda other: mid.at[which, pl.ds(other * per, per)], got2.at[which, me])

    def added(ref, which, count):
        totals = [ref[which, i].astype(F32) for i in range(count)]
        while len(totals) > 1:
            totals = [a + b for a, b in zip(totals[::2], totals[1::2])]
        return totals[0].astype(BF16)

    def reduce_deep(which, copies):
        arrive(copies)
        got3[which, depth] = added(got2, which, len(offsets) + 1)
        mine = got3.at[which, depth]
        return to_depths(which, mine, mine)

    def gather_members(which, copies):
        arrive(copies)
        sums[which, core, pl.ds(me * per, per)] = added(got3, which, deep)
        mine = mine_of(which)
        return to_members(1, which, lambda other: mine, mine)

    def gather_pair(which, copies):
        arrive(copies)
        mine = sums.at[which, core, 0:pad]
        return to_twin(1, which, mine, mine)

    factor = float(n_x * CORES * space * n) ** (-0.5)

    def lay_out(which, side, out):
        for i in range(pad):
            tile = side * pad + i
            k = tile // 2
            value = sums[which, side, i].astype(F32) * factor
            top = pl.multiple_of(tile % 2 * TILE, TILE)
            out[k, pl.ds(top, TILE), :] = value[:, :C]
            out[k, pl.ds(top + C // 2, TILE), :] = value[:, C:]

    def drain(copies):
        for copy in copies:
            copy.wait_send()

    one = reduce_pair(0)
    sent += one
    fill_own(table2, hid)
    relay_wait(2)
    relay_signal(3)
    w2t[...] = w2_ref[...].T
    relay_wait(3)
    one = scatter_reduce(0, one)
    sent += one
    arrive(hid_copies)
    fill_halo(table2, halo_mid)
    pick(table2, picked2)
    weight_parts(1, picked2, cot)
    two = reduce_pair(1)
    sent += two

    spread(w1_ref, grad_pre)
    two = scatter_reduce(1, two)
    sent += two
    rim = scattered(n).astype(BF16)
    for i in range(2):
        rim_out[1, i] = rim[:, i * half : (i + 1) * half]
    last_copies = to_neighbours(3, rim_out.at[1, 0], rim_out.at[1, 1], rim_in.at[1])
    sent += last_copies
    from_channels(convolved(w2t, picked2).astype(BF16), conv_ref)

    relay_end()
    one = reduce_deep(0, one)
    sent += one
    grad_in = scattered(0)
    two = reduce_deep(1, two)
    sent += two
    arrive(last_copies)
    rims = jnp.concatenate([rim_in[1, 0], rim_in[1, 1]], axis=1).astype(F32)
    from_channels((grad_in + rims).astype(BF16), gin_ref)
    drain(sent)

    one = gather_members(0, one)
    sent = list(one)
    two = gather_members(1, two)
    sent += two
    one = gather_pair(0, one)
    sent += one
    lay_out(0, core, grad1_ref)
    arrive(one)
    lay_out(0, 1 - core, grad1_ref)
    two = gather_pair(1, two)
    drain(sent)
    lay_out(1, core, grad2_ref)
    arrive(two)
    lay_out(1, 1 - core, grad2_ref)
    drain(two)


def put_kernel(*refs):
    count = len(refs) // 2
    sem = refs[-1]
    copies = []
    for i, (src, dst) in enumerate(zip(refs[:count], refs[count:-1])):
        size = src.shape[0]
        cuts = 3 if size == K else 1
        for c in range(cuts):
            part = pl.ds(c * size // cuts, size // cuts)
            copies.append(pltpu.make_async_copy(src.at[part], dst.at[part], sem.at[i, c]))
    for copy in copies:
        copy.start()
    for copy in copies:
        copy.wait()


def per_device(sizes, features, sources, voxels, cotangent, weight_one, weight_two):
    n_x, n_y, n_z = sizes
    members = n_x * n_y * ZPAR
    deep = n_z // ZPAR
    blocks = features.shape[1]
    n = blocks * V
    half = n // 2
    pad = TILES // CORES
    per = -(-pad // members)
    slots = blocks + 2 * HALO
    scratch = [
        pltpu.VMEM((blocks, V * C), BF16),
        pltpu.VMEM((blocks, V * C), BF16),
        pltpu.SMEM((blocks, K), jnp.int32),
        pltpu.VMEM((blocks, K * V), jnp.int32),
        pltpu.VMEM((K * C, C), BF16),
        pltpu.VMEM((K * C, C), BF16),
        pltpu.SMEM((K * blocks,), jnp.int32),
        pltpu.VMEM((K, 1, n), F32),
        pltpu.VMEM((K, 1, n), F32),
        pltpu.VMEM((n // 2, 2 * C), F32),
        pltpu.VMEM((blocks, V * C), F32),
        pltpu.VMEM((slots, C, 2 * V), BF16),
        pltpu.VMEM((slots, C, 2 * V), BF16),
        pltpu.VMEM((C, n), BF16),
        pltpu.VMEM((K, C, n), BF16),
        pltpu.VMEM((K, C, n), BF16),
        pltpu.VMEM((K, C, n), BF16),
        pltpu.VMEM((C, K * C), BF16),
        pltpu.VMEM((C, K * C), BF16),
        pltpu.VMEM((2, C, half), BF16),
        pltpu.VMEM((2, C, half), BF16),
        pltpu.VMEM((2, 2, C, half), BF16),
        pltpu.VMEM((2, 2, C, half), BF16),
        pltpu.VMEM((C, n), BF16),
        pltpu.VMEM((2, CORES, pad, TILE, 2 * C), BF16),
        pltpu.VMEM((2, pad, TILE, 2 * C), BF16),
        pltpu.VMEM((2, members * per, TILE, 2 * C), BF16),
        pltpu.VMEM((2, members, per, TILE, 2 * C), BF16),
        pltpu.VMEM((2, deep, per, TILE, 2 * C), BF16),
        pltpu.VMEM((2, CORES, members * per, TILE, 2 * C), BF16),
        pltpu.SemaphoreType.DMA((6,)),
        pltpu.SemaphoreType.DMA((4, 2)),
        pltpu.SemaphoreType.DMA((4, 2)),
        pltpu.SemaphoreType.DMA((2, 2)),
        pltpu.SemaphoreType.DMA((2, 2)),
        pltpu.SemaphoreType.DMA((2, 2, members - 1)),
        pltpu.SemaphoreType.DMA((2, 2, members - 1)),
        pltpu.SemaphoreType.DMA((2, deep - 1)),
        pltpu.SemaphoreType.DMA((2, deep - 1)),
        pltpu.SemaphoreType.REGULAR((8,)),
    ]
    outs = (
        jax.ShapeDtypeStruct((blocks, V * C), BF16),
        jax.ShapeDtypeStruct((blocks, V * C), BF16),
        jax.ShapeDtypeStruct((K, C, C), F32),
        jax.ShapeDtypeStruct((K, C, C), F32),
    )
    vmem = pl.BlockSpec(memory_space=pltpu.VMEM)
    anywhere = pl.BlockSpec(memory_space=pl.ANY)
    hbm = pl.BlockSpec(memory_space=pltpu.HBM)
    results = pl.pallas_call(
        functools.partial(step_kernel, sizes),
        out_shape=outs,
        in_specs=[hbm] * 6,
        out_specs=(vmem,) * 4,
        scratch_shapes=scratch,
        compiler_params=pltpu.CompilerParams(
            collective_id=0, has_side_effects=True, vmem_limit_bytes=32 * 1024 * 1024
        ),
        name="step",
    )(
        features[0],
        cotangent[0],
        sources[0],
        voxels[0],
        weight_one.reshape(K * C, C),
        weight_two.reshape(K * C, C),
    )
    conv, gin, grad_one, grad_two = pl.pallas_call(
        put_kernel,
        out_shape=outs,
        in_specs=[anywhere] * 4,
        out_specs=(hbm,) * 4,
        scratch_shapes=[pltpu.SemaphoreType.DMA((4, 3))],
        compiler_params=pltpu.CompilerParams(vmem_limit_bytes=1024 * 1024),
        name="put",
    )(*results)
    return conv[None], gin[None], grad_one, grad_two


def solution(mesh):
    space, dp = mesh.shape["space"], mesh.shape["dp"]
    sizes = (dp // CORES, Y, space // Y)
    wide = P("dp", "space", None)
    return jax.shard_map(
        functools.partial(per_device, sizes),
        mesh=mesh,
        in_specs=(wide, wide, wide, wide, P(), P()),
        out_specs=(wide, wide, P(), P()),
        check_vma=False,
    )
```

time: 60.1 us -> 55.2 us (0.918)
  local copies, waits for them, and re-layouts: 8.61 us -> 4.96 us
  other arithmetic: 0.91 us -> 0 us
    unnamed x6 -> x12, local copies, waits for them, and re-layouts: 1.66 us -> 4.96 us
    mul x4 -> x0, local copies, waits for them, and re-layouts: 3.08 us -> none  [whole(): jnp.transpose(pairs, (0, 2, 1, 3)).reshape(K, C, C).astype(F32) * factor]
    another operation x5 -> x0, local copies, waits for them, and re-layouts: 2.02 us -> none  [the longest x2 0.97 us: per_device(): feat = features[0].reshape(n, C).T]
    reshape x3 -> x0, local copies, waits for them, and re-layouts: 1.58 us -> none  [the longest x1 0.74 us: per_device(): conv = conv.T.reshape(1, blocks, V * C)]
    mul x2 -> x0, other arithmetic: 0.83 us -> none  [the longest x1 0.75 us: per_device(): rows = jnp.where(vox == V, -1, slot[:, :, None] * V + vox)]
    pallas_call x1 -> x2, Pallas kernels: 49.5 us -> 49.2 us  [the longest x1 47.8 us: per_device(): pl.pallas_call(functools.partial(step_kernel, sizes), out_shape=outs, in_...]
where the time goes in v3:
time: 55.2 us; the launch traced here: 54.8 us
  Pallas kernels  49.2 us (89%)
  local copies, waits for them, and re-layouts  4.96 us (9%)
  between operations  0.65 us (1%)
    pallas_call x1, Pallas kernels, per_device(): pl.pallas_call(functools.partial(step_kernel, sizes), out_shape=outs, in_...  47.8 us
    unnamed x12, local copies, waits for them, and re-layouts  4.96 us
    pallas_call x1, Pallas kernels, per_device(): pl.pallas_call(put_kernel, out_shape=outs, in_specs=[anywhere] * 4, out_s...  1.33 us

profile of v3, /device:TPU:1, one launch (start us, length us, event | category | flops | bytes accessed | tf_op | source)
XLA Modules:
  0.0 54.8 jit_solution(5681446611786056313)
XLA Ops:
  0.6 0.0 copy-start.5
  0.6 0.7 %copy-done.5 = s32[1,4,27]{2,1,0:T(4,128)S(1)} copy-done((s32[1,4,27]{2,1,0:T(4,128)S(1)}, s32[1,4,27]{2,1,0:T(4,128)}, u32[]{:S(2)}) %copy-start.5) | copy-done | bytes 456
  1.3 0.0 copy-start
  1.3 1.0 %copy-done = bf16[27,64,64]{2,1,0:T(8,128)(2,1)S(1)} copy-done((bf16[27,64,64]{2,1,0:T(8,128)(2,1)S(1)}, bf16[27,64,64]{2,1,0:T(8,128)(2,1)}, u32[]{:S(2)}) %copy-start) | copy-done | bytes 221208
  2.3 0.0 copy-start.1
  2.3 1.0 %copy-done.1 = bf16[27,64,64]{2,1,0:T(8,128)(2,1)S(1)} copy-done((bf16[27,64,64]{2,1,0:T(8,128)(2,1)S(1)}, bf16[27,64,64]{2,1,0:T(8,128)(2,1)}, u32[]{:S(2)}) %copy-start.1) | copy-done | bytes 221208
  3.3 0.0 copy-start.2
  3.3 0.8 %copy-done.2 = bf16[1,4,4096]{2,1,0:T(4,128)(2,1)S(1)} copy-done((bf16[1,4,4096]{2,1,0:T(4,128)(2,1)S(1)}, bf16[1,4,4096]{2,1,0:T(4,128)(2,1)}, u32[]{:S(2)}) %copy-start.2) | copy-done | bytes 32792
  4.1 0.0 copy-start.3
  4.1 0.8 %copy-done.3 = bf16[1,4,4096]{2,1,0:T(4,128)(2,1)S(1)} copy-done((bf16[1,4,4096]{2,1,0:T(4,128)(2,1)S(1)}, bf16[1,4,4096]{2,1,0:T(4,128)(2,1)}, u32[]{:S(2)}) %copy-start.3) | copy-done | bytes 32792
  4.9 0.0 copy-start.4
  4.9 0.7 %copy-done.4 = s32[1,4,1728]{2,1,0:T(4,128)S(1)} copy-done((s32[1,4,1728]{2,1,0:T(4,128)S(1)}, s32[1,4,1728]{2,1,0:T(4,128)}, u32[]{:S(2)}) %copy-start.4) | copy-done | bytes 27672
  5.6 47.8 %step.1 = (bf16[4,4096]{1,0:T(4,128)(2,1)S(1)}, bf16[4,4096]{1,0:T(4,128)(2,1)S(1)}, f32[27,64,64]{2,1,0:T(8,128)S(1)}, f32[27,64,64]{2,1,0:T(8,128)S(1)}) custom-call(bf16[4,4096]{1,0:T(4,128)(2,1)S(1)} %bitcast.10, bf16[4,4096]{1,0:T(4,128)(2,1)S(1)} %bitcast.11, s32[4,27]{1,0:T(4,128)S(1)} %bitcast.13, s32[4,1728]{1,0:T(4,128)S(1)} %bitcast.12, ...), custom_call_target="tpu_custom_call" | custom-call | tf_op jit(solution)/shard_map/step/pallas_call | solution.py:559
  53.4 1.3 %put.1 = (bf16[4,4096]{1,0:T(4,128)(2,1)}, bf16[4,4096]{1,0:T(4,128)(2,1)}, f32[27,64,64]{2,1,0:T(8,128)}, f32[27,64,64]{2,1,0:T(8,128)}) custom-call(bf16[4,4096]{1,0:T(4,128)(2,1)S(1)} %get-tuple-element.12.refs_0_, bf16[4,4096]{1,0:T(4,128)(2,1)S(1)} %get-tuple-element.13.refs_1_, f32[27,64,64]{2,1,0:T(8,128)S(1)} %get-tuple-element.14.refs_2_, ...), custom_call_target="tpu_custom_call" | custom-call | tf_op jit(solution)/shard_map/put/pallas_call | solution.py:577
Async XLA Ops:
  0.6 0.7 %copy-start.5 = (s32[1,4,27]{2,1,0:T(4,128)S(1)}, s32[1,4,27]{2,1,0:T(4,128)}, u32[]{:S(2)}) copy-start(s32[1,4,27]{2,1,0:T(4,128)} %param.7) | copy-start | bytes 1300
  1.3 1.0 %copy-start = (bf16[27,64,64]{2,1,0:T(8,128)(2,1)S(1)}, bf16[27,64,64]{2,1,0:T(8,128)(2,1)}, u32[]{:S(2)}) copy-start(bf16[27,64,64]{2,1,0:T(8,128)(2,1)} %param.10) | copy-start | bytes 663556
  2.3 1.0 %copy-start.1 = (bf16[27,64,64]{2,1,0:T(8,128)(2,1)S(1)}, bf16[27,64,64]{2,1,0:T(8,128)(2,1)}, u32[]{:S(2)}) copy-start(bf16[27,64,64]{2,1,0:T(8,128)(2,1)} %param.11) | copy-start | bytes 663556
  3.3 0.8 %copy-start.2 = (bf16[1,4,4096]{2,1,0:T(4,128)(2,1)S(1)}, bf16[1,4,4096]{2,1,0:T(4,128)(2,1)}, u32[]{:S(2)}) copy-start(bf16[1,4,4096]{2,1,0:T(4,128)(2,1)} %param.6) | copy-start | bytes 98308
  4.1 0.8 %copy-start.3 = (bf16[1,4,4096]{2,1,0:T(4,128)(2,1)S(1)}, bf16[1,4,4096]{2,1,0:T(4,128)(2,1)}, u32[]{:S(2)}) copy-start(bf16[1,4,4096]{2,1,0:T(4,128)(2,1)} %param.9) | copy-start | bytes 98308
  4.9 0.7 %copy-start.4 = (s32[1,4,1728]{2,1,0:T(4,128)S(1)}, s32[1,4,1728]{2,1,0:T(4,128)}, u32[]{:S(2)}) copy-start(s32[1,4,1728]{2,1,0:T(4,128)} %param.8) | copy-start | bytes 82948

commit v4 on v3

--- a/solution.py
+++ b/solution.py
@@ -567,12 +567,17 @@
         ),
         name="step",
     )(
-        features[0],
-        cotangent[0],
-        sources[0],
-        voxels[0],
-        weight_one.reshape(K * C, C),
-        weight_two.reshape(K * C, C),
+        *[
+            pltpu.with_memory_space_constraint(a, pltpu.HBM)
+            for a in (
+                features[0],
+                cotangent[0],
+                sources[0],
+                voxels[0],
+                weight_one.reshape(K * C, C),
+                weight_two.reshape(K * C, C),
+            )
+        ]
     )
     conv, gin, grad_one, grad_two = pl.pallas_call(
         put_kernel,

time: 55.2 us -> 49.9 us (0.904)
  local copies, waits for them, and re-layouts: 4.96 us -> 0 us
    unnamed x12 -> x0, local copies, waits for them, and re-layouts: 4.96 us -> none
where the time goes in v4:
time: 49.9 us; the launch traced here: 49.8 us
  Pallas kernels  49.2 us (99%)
  between operations  0.64 us (1%)
    pallas_call x1, Pallas kernels, per_device(): pl.pallas_call(functools.partial(step_kernel, sizes), out_shape=outs, in_...  47.8 us
    pallas_call x1, Pallas kernels, per_device(): pl.pallas_call(put_kernel, out_shape=outs, in_specs=[anywhere] * 4, out_s...  1.33 us

profile of v4, /device:TPU:1, one launch (start us, length us, event | category | flops | bytes accessed | tf_op | source)
XLA Modules:
  0.0 49.8 jit_solution(7609502008149514490)
XLA Ops:
  0.6 47.8 %step.1 = (bf16[4,4096]{1,0:T(4,128)(2,1)S(1)}, bf16[4,4096]{1,0:T(4,128)(2,1)S(1)}, f32[27,64,64]{2,1,0:T(8,128)S(1)}, f32[27,64,64]{2,1,0:T(8,128)S(1)}) custom-call(bf16[4,4096]{1,0:T(4,128)(2,1)} %bitcast.10, bf16[4,4096]{1,0:T(4,128)(2,1)} %bitcast.11, s32[4,27]{1,0:T(4,128)} %bitcast.13, s32[4,1728]{1,0:T(4,128)} %bitcast.12, ...), custom_call_target="tpu_custom_call" | custom-call | tf_op jit(solution)/shard_map/step/pallas_call | solution.py:559
  48.5 1.3 %put.1 = (bf16[4,4096]{1,0:T(4,128)(2,1)}, bf16[4,4096]{1,0:T(4,128)(2,1)}, f32[27,64,64]{2,1,0:T(8,128)}, f32[27,64,64]{2,1,0:T(8,128)}) custom-call(bf16[4,4096]{1,0:T(4,128)(2,1)S(1)} %get-tuple-element.12.refs_0_, bf16[4,4096]{1,0:T(4,128)(2,1)S(1)} %get-tuple-element.13.refs_1_, f32[27,64,64]{2,1,0:T(8,128)S(1)} %get-tuple-element.14.refs_2_, ...), custom_call_target="tpu_custom_call" | custom-call | tf_op jit(solution)/shard_map/put/pallas_call | solution.py:582

commit v5 on v4

--- a/solution.py
+++ b/solution.py
@@ -280,14 +280,22 @@
             if cut < tiles:
                 parts[which, 1, first + cut - pad : first + tiles - pad] = out[cut:]
 
+    class Batch:
+        def __init__(self, copies, send, recv, sent, landed):
+            for copy in copies:
+                copy.start()
+            self.all = remote(sent, landed, send, recv, twin)
+
+        def wait_recv(self):
+            self.all.wait_recv()
+
+        def wait_send(self):
+            self.all.wait_send()
+
     def to_neighbours(slot, low, high, into):
-        copies = [
-            remote(low, into.at[1], halo_send.at[slot, 0], halo_recv.at[slot, 1], before),
-            remote(high, into.at[0], halo_send.at[slot, 1], halo_recv.at[slot, 0], after),
-        ]
-        for copy in copies:
-            copy.start()
-        return copies
+        send, recv = halo_send.at[slot], halo_recv.at[slot]
+        copies = [remote(low, into.at[1], send, recv, before), remote(high, into.at[0], send, recv, after)]
+        return [Batch(copies, send, recv, into, into)]
 
     def arrive(copies):
         for copy in copies:
@@ -308,26 +316,22 @@
         copy.start()
         return [copy]
 
-    def to_members(stage, which, src_of, dst):
+    def to_members(stage, which, src_of, dst, all_of):
+        send, recv = group_send.at[stage, which], group_recv.at[stage, which]
         copies = []
-        for i, (dx, dy, dz) in enumerate(offsets):
+        for dx, dy, dz in offsets:
             xx, yy, zz = (x + dx) % n_x, (y + dy) % n_y, (z_par + dz) % ZPAR
             target = (((z // ZPAR) * ZPAR + zz) * n_y + yy, xx * CORES + core)
-            copy = remote(
-                src_of(member(xx, yy, zz)), dst, group_send.at[stage, which, i], group_recv.at[stage, which, i], target
-            )
-            copy.start()
-            copies.append(copy)
-        return copies
+            copies.append(remote(src_of(member(xx, yy, zz)), dst, send, recv, target))
+        return [Batch(copies, send, recv, all_of, all_of)]
 
     def to_depths(which, src, dst):
+        send, recv = deep_send.at[which], deep_recv.at[which]
         copies = []
         for j in [j for i in range(deep // 2, 0, -1) for j in sorted({i, deep - i})]:
-            target = at(dz=j * ZPAR)
-            copy = remote(src, dst, deep_send.at[which, j - 1], deep_recv.at[which, j - 1], target)
-            copy.start()
-            copies.append(copy)
-        return copies
+            copies.append(remote(src, dst, send, recv, at(dz=j * ZPAR)))
+        every = got3.at[which, 0 : deep - 1]
+        return [Batch(copies, send, recv, every, every)]
 
     for which in range(2):
         mid[which, pad:] = jnp.zeros((mid.shape[1] - pad, TILE, 2 * C), BF16)
@@ -385,7 +389,10 @@
         arrive(copies)
         mid[which, 0:pad] = (parts[which, core].astype(F32) + got1[which].astype(F32)).astype(BF16)
         got2[which, me] = mid[which, pl.ds(me * per, per)]
-        return to_members(0, which, lambda other: mid.at[which, pl.ds(other * per, per)], got2.at[which, me])
+        every = got2.at[which, 0 : len(offsets)]
+        return to_members(
+            0, which, lambda other: mid.at[which, pl.ds(other * per, per)], got2.at[which, me], every
+        )
 
     def added(ref, which, count):
         totals = [ref[which, i].astype(F32) for i in range(count)]
@@ -403,7 +410,8 @@
         arrive(copies)
         sums[which, core, pl.ds(me * per, per)] = added(got3, which, deep)
         mine = mine_of(which)
-        return to_members(1, which, lambda other: mine, mine)
+        every = sums.at[which, core, 0 : len(offsets) * per]
+        return to_members(1, which, lambda other: mine, mine, every)
 
     def gather_pair(which, copies):
         arrive(copies)
@@ -457,15 +465,14 @@
     grad_in = scattered(0)
     two = reduce_deep(1, two)
     sent += two
+    one = gather_members(0, one)
+    sent += one
     arrive(last_copies)
     rims = jnp.concatenate([rim_in[1, 0], rim_in[1, 1]], axis=1).astype(F32)
-    from_channels((grad_in + rims).astype(BF16), gin_ref)
-    drain(sent)
-
-    one = gather_members(0, one)
-    sent = list(one)
+    grad_input = (grad_in + rims).astype(BF16)
     two = gather_members(1, two)
     sent += two
+    from_channels(grad_input, gin_ref)
     one = gather_pair(0, one)
     sent += one
     lay_out(0, core, grad1_ref)
@@ -537,15 +544,15 @@
         pltpu.VMEM((2, deep, per, TILE, 2 * C), BF16),
         pltpu.VMEM((2, CORES, members * per, TILE, 2 * C), BF16),
         pltpu.SemaphoreType.DMA((6,)),
-        pltpu.SemaphoreType.DMA((4, 2)),
-        pltpu.SemaphoreType.DMA((4, 2)),
+        pltpu.SemaphoreType.DMA((4,)),
+        pltpu.SemaphoreType.DMA((4,)),
         pltpu.SemaphoreType.DMA((2, 2)),
         pltpu.SemaphoreType.DMA((2, 2)),
-        pltpu.SemaphoreType.DMA((2, 2, members - 1)),
-        pltpu.SemaphoreType.DMA((2, 2, members - 1)),
-        pltpu.SemaphoreType.DMA((2, deep - 1)),
-        pltpu.SemaphoreType.DMA((2, deep - 1)),
-        pltpu.SemaphoreType.REGULAR((8,)),
+        pltpu.SemaphoreType.DMA((2, 2)),
+        pltpu.SemaphoreType.DMA((2, 2)),
+        pltpu.SemaphoreType.DMA((2,)),
+        pltpu.SemaphoreType.DMA((2,)),
+        pltpu.SemaphoreType.REGULAR((7,)),
     ]
     outs = (
         jax.ShapeDtypeStruct((blocks, V * C), BF16),

time: 49.9 us -> 47.5 us (0.952)
  Pallas kernels: 49.2 us -> 46.7 us
    pallas_call x1, Pallas kernels: 47.8 us -> 45.4 us  [per_device(): pl.pallas_call(functools.partial(step_kernel, sizes), out_shape=outs, in_...]
where the time goes in v5:
time: 47.5 us; the launch traced here: 47.3 us
  Pallas kernels  46.7 us (98%)
  between operations  0.64 us (1%)
    pallas_call x1, Pallas kernels, per_device(): pl.pallas_call(functools.partial(step_kernel, sizes), out_shape=outs, in_...  45.4 us
    pallas_call x1, Pallas kernels, per_device(): pl.pallas_call(put_kernel, out_shape=outs, in_specs=[anywhere] * 4, out_s...  1.33 us

profile of v5, /device:TPU:1, one launch (start us, length us, event | category | flops | bytes accessed | tf_op | source)
XLA Modules:
  0.0 47.3 jit_solution(5788353397981475700)
XLA Ops:
  0.6 45.4 %step.1 = (bf16[4,4096]{1,0:T(4,128)(2,1)S(1)}, bf16[4,4096]{1,0:T(4,128)(2,1)S(1)}, f32[27,64,64]{2,1,0:T(8,128)S(1)}, f32[27,64,64]{2,1,0:T(8,128)S(1)}) custom-call(bf16[4,4096]{1,0:T(4,128)(2,1)} %bitcast.10, bf16[4,4096]{1,0:T(4,128)(2,1)} %bitcast.11, s32[4,27]{1,0:T(4,128)} %bitcast.13, s32[4,1728]{1,0:T(4,128)} %bitcast.12, ...), custom_call_target="tpu_custom_call" | custom-call | tf_op jit(solution)/shard_map/step/pallas_call | solution.py:566
  46.0 1.3 %put.1 = (bf16[4,4096]{1,0:T(4,128)(2,1)}, bf16[4,4096]{1,0:T(4,128)(2,1)}, f32[27,64,64]{2,1,0:T(8,128)}, f32[27,64,64]{2,1,0:T(8,128)}) custom-call(bf16[4,4096]{1,0:T(4,128)(2,1)S(1)} %get-tuple-element.12.refs_0_, bf16[4,4096]{1,0:T(4,128)(2,1)S(1)} %get-tuple-element.13.refs_1_, f32[27,64,64]{2,1,0:T(8,128)S(1)} %get-tuple-element.14.refs_2_, ...), custom_call_target="tpu_custom_call" | custom-call | tf_op jit(solution)/shard_map/put/pallas_call | solution.py:589

commit v6 on v5

--- a/solution.py
+++ b/solution.py
@@ -15,7 +15,8 @@
 ZPAR = 2
 CORES = 2
 TILE = 16
-TILES = K * C * C // (TILE * 2 * C)
+K_EVEN = K + K % 2
+TILES = K_EVEN * C * C // (TILE * 2 * C)
 MESH = pl.DeviceIdType.MESH
 BF16 = jnp.bfloat16
 F32 = jnp.float32
@@ -54,6 +55,8 @@
     picked1,
     picked2,
     back,
+    spreads,
+    w2p,
     w1t,
     w2t,
     halo_in,
@@ -227,6 +230,33 @@
 
         return lax.fori_loop(0, K // group_of, some, jnp.zeros((C, n), F32))
 
+    def spread_out(grad, side):
+        def some(g, carry):
+            for i in range(group_of):
+                k = g * group_of + i
+                out = mxu(grad, hot(spot, wide_rows[k] - side * n), ((1,), (1,)))
+                spreads[k, :, side * n : (side + 1) * n] = out.astype(BF16)
+            return carry
+
+        lax.fori_loop(0, K // group_of, some, 0)
+
+    def gathered_back(side):
+        return mxu(w2p[:, 0 : K * C], spreads[0:K, :, side * n : (side + 1) * n].reshape(K * C, n))
+
+    def pair_weights():
+        for k in range(0, K_EVEN, 2):
+            first = w2_ref[k * C : (k + 1) * C, :]
+            second = w2_ref[(k + 1) * C : (k + 2) * C, :] if k + 1 < K else jnp.zeros_like(first)
+            w2p[:, k * C : (k + 2) * C] = jnp.concatenate([first, second], axis=1)
+
+    def weight_parts_wide(which, table):
+        for g in range(0, K_EVEN, 4):
+            out = mxu(table, spreads[g : g + 4].reshape(4 * C, 2 * n), ((1,), (1,))).astype(BF16)
+            for j in range(2):
+                rows = out[:, j * 2 * C : (j + 1) * 2 * C].reshape(C // TILE, TILE, 2 * C)
+                first = (g // 2 + j) * (C // TILE)
+                parts[which, first // pad, first % pad : first % pad + C // TILE] = rows
+
     low16 = iota((C, 2 * V), 1).astype(F32).astype(BF16) < V
     low32 = iota((C, 2 * V), 1) < V
 
@@ -333,6 +363,9 @@
         every = got3.at[which, 0 : deep - 1]
         return [Batch(copies, send, recv, every, every)]
 
+    spreads[K:] = jnp.zeros((K_EVEN - K, C, 2 * n), BF16)
+    used = K * C // 2 // TILE - pad
+    parts[0, 1, used:] = jnp.zeros((pad - used, TILE, 2 * C), BF16)
     for which in range(2):
         mid[which, pad:] = jnp.zeros((mid.shape[1] - pad, TILE, 2 * C), BF16)
     loads["x"].wait()
@@ -348,9 +381,10 @@
     make_rows()
     loads["ct"].wait()
     cot = to_channels(ct_ref)
+    spread_out(cot, 1)
     loads["w2"].wait()
-    spread(w2_ref, cot)
-    rim = scattered(n).astype(BF16)
+    pair_weights()
+    rim = gathered_back(1).astype(BF16)
     for i in range(2):
         rim_out[0, i] = rim[:, i * half : (i + 1) * half]
     rim_copies = to_neighbours(1, rim_out.at[0, 0], rim_out.at[0, 1], rim_in.at[0])
@@ -373,7 +407,8 @@
     relay_wait(1)
     relay_signal(2)
 
-    grad_hidden = scattered(0)
+    spread_out(cot, 0)
+    grad_hidden = gathered_back(0)
     arrive(rim_copies)
     rims = jnp.concatenate([rim_in[0, 0], rim_in[0, 1]], axis=1).astype(F32)
     grad_pre = ((grad_hidden + rims) * (sig * (1.0 + pre * (1.0 - sig)))).astype(BF16)
@@ -423,11 +458,15 @@
     def lay_out(which, side, out):
         for i in range(pad):
             tile = side * pad + i
-            k = tile // 2
             value = sums[which, side, i].astype(F32) * factor
-            top = pl.multiple_of(tile % 2 * TILE, TILE)
-            out[k, pl.ds(top, TILE), :] = value[:, :C]
-            out[k, pl.ds(top + C // 2, TILE), :] = value[:, C:]
+            if which == 0:
+                k, top = tile // 2, pl.multiple_of(tile % 2 * TILE, TILE)
+                out[k, pl.ds(top, TILE), :] = value[:, :C]
+                out[k, pl.ds(top + C // 2, TILE), :] = value[:, C:]
+            else:
+                k, top = tile // 4 * 2, pl.multiple_of(tile % 4 * TILE, TILE)
+                out[k, pl.ds(top, TILE), :] = value[:, :C]
+                out[k + 1, pl.ds(top, TILE), :] = value[:, C:]
 
     def drain(copies):
         for copy in copies:
@@ -435,7 +474,6 @@
 
     one = reduce_pair(0)
     sent += one
-    fill_own(table2, hid)
     relay_wait(2)
     relay_signal(3)
     w2t[...] = w2_ref[...].T
@@ -443,26 +481,27 @@
     one = scatter_reduce(0, one)
     sent += one
     arrive(hid_copies)
-    fill_halo(table2, halo_mid)
-    pick(table2, picked2)
-    weight_parts(1, picked2, cot)
+    weight_parts_wide(1, jnp.concatenate([hid, halo_mid[0], halo_mid[1]], axis=1))
     two = reduce_pair(1)
     sent += two
 
     spread(w1_ref, grad_pre)
-    two = scatter_reduce(1, two)
-    sent += two
     rim = scattered(n).astype(BF16)
     for i in range(2):
         rim_out[1, i] = rim[:, i * half : (i + 1) * half]
     last_copies = to_neighbours(3, rim_out.at[1, 0], rim_out.at[1, 1], rim_in.at[1])
     sent += last_copies
+    two = scatter_reduce(1, two)
+    sent += two
+    fill_own(table2, hid)
+    fill_halo(table2, halo_mid)
+    pick(table2, picked2)
     from_channels(convolved(w2t, picked2).astype(BF16), conv_ref)
+    grad_in = scattered(0)
 
     relay_end()
     one = reduce_deep(0, one)
     sent += one
-    grad_in = scattered(0)
     two = reduce_deep(1, two)
     sent += two
     one = gather_members(0, one)
@@ -491,7 +530,7 @@
     sem = refs[-1]
     copies = []
     for i, (src, dst) in enumerate(zip(refs[:count], refs[count:-1])):
-        size = src.shape[0]
+        size = dst.shape[0]
         cuts = 3 if size == K else 1
         for c in range(cuts):
             part = pl.ds(c * size // cuts, size // cuts)
@@ -530,6 +569,8 @@
         pltpu.VMEM((K, C, n), BF16),
         pltpu.VMEM((K, C, n), BF16),
         pltpu.VMEM((K, C, n), BF16),
+        pltpu.VMEM((K_EVEN, C, 2 * n), BF16),
+        pltpu.VMEM((C, K_EVEN * C), BF16),
         pltpu.VMEM((C, K * C), BF16),
         pltpu.VMEM((C, K * C), BF16),
         pltpu.VMEM((2, C, half), BF16),
@@ -563,9 +604,10 @@
     vmem = pl.BlockSpec(memory_space=pltpu.VMEM)
     anywhere = pl.BlockSpec(memory_space=pl.ANY)
     hbm = pl.BlockSpec(memory_space=pltpu.HBM)
+    even = jax.ShapeDtypeStruct((K_EVEN, C, C), F32)
     results = pl.pallas_call(
         functools.partial(step_kernel, sizes),
-        out_shape=outs,
+        out_shape=(*outs[:2], even, even),
         in_specs=[hbm] * 6,
         out_specs=(vmem,) * 4,
         scratch_shapes=scratch,

time: 47.5 us -> 48 us (1.011)
  Pallas kernels: 46.7 us -> 47.3 us
    pallas_call x1, Pallas kernels: 45.4 us -> 45.9 us  [per_device(): pl.pallas_call(functools.partial(step_kernel, sizes), out_shape=(*outs[:2...]
where the time goes in v6:
time: 48 us; the launch traced here: 47.9 us
  Pallas kernels  47.3 us (99%)
  between operations  0.64 us (1%)
    pallas_call x1, Pallas kernels, per_device(): pl.pallas_call(functools.partial(step_kernel, sizes), out_shape=(*outs[:2...  45.9 us
    pallas_call x1, Pallas kernels, per_device(): pl.pallas_call(put_kernel, out_shape=outs, in_specs=[anywhere] * 4, out_s...  1.33 us

profile of v6, /device:TPU:1, one launch (start us, length us, event | category | flops | bytes accessed | tf_op | source)
XLA Modules:
  0.0 47.9 jit_solution(7331914414737101774)
XLA Ops:
  0.6 45.9 %step.1 = (bf16[4,4096]{1,0:T(4,128)(2,1)S(1)}, bf16[4,4096]{1,0:T(4,128)(2,1)S(1)}, f32[28,64,64]{2,1,0:T(8,128)S(1)}, f32[28,64,64]{2,1,0:T(8,128)S(1)}) custom-call(bf16[4,4096]{1,0:T(4,128)(2,1)} %bitcast.10, bf16[4,4096]{1,0:T(4,128)(2,1)} %bitcast.11, s32[4,27]{1,0:T(4,128)} %bitcast.13, s32[4,1728]{1,0:T(4,128)} %bitcast.12, ...), custom_call_target="tpu_custom_call" | custom-call | tf_op jit(solution)/shard_map/step/pallas_call | solution.py:608
  46.6 1.3 %put.1 = (bf16[4,4096]{1,0:T(4,128)(2,1)}, bf16[4,4096]{1,0:T(4,128)(2,1)}, f32[27,64,64]{2,1,0:T(8,128)}, f32[27,64,64]{2,1,0:T(8,128)}) custom-call(bf16[4,4096]{1,0:T(4,128)(2,1)S(1)} %get-tuple-element.12.refs_0_, bf16[4,4096]{1,0:T(4,128)(2,1)S(1)} %get-tuple-element.13.refs_1_, f32[28,64,64]{2,1,0:T(8,128)S(1)} %get-tuple-element.14.refs_2_, ...), custom_call_target="tpu_custom_call" | custom-call | tf_op jit(solution)/shard_map/put/pallas_call | solution.py:631

commit v7 on v6

--- a/solution.py
+++ b/solution.py
@@ -486,24 +486,24 @@
     sent += two
 
     spread(w1_ref, grad_pre)
+    two = scatter_reduce(1, two)
+    sent += two
     rim = scattered(n).astype(BF16)
     for i in range(2):
         rim_out[1, i] = rim[:, i * half : (i + 1) * half]
     last_copies = to_neighbours(3, rim_out.at[1, 0], rim_out.at[1, 1], rim_in.at[1])
     sent += last_copies
-    two = scatter_reduce(1, two)
-    sent += two
+    relay_end()
+    one = reduce_deep(0, one)
+    sent += one
     fill_own(table2, hid)
     fill_halo(table2, halo_mid)
     pick(table2, picked2)
     from_channels(convolved(w2t, picked2).astype(BF16), conv_ref)
-    grad_in = scattered(0)
-
-    relay_end()
-    one = reduce_deep(0, one)
-    sent += one
     two = reduce_deep(1, two)
     sent += two
+    grad_in = scattered(0)
+
     one = gather_members(0, one)
     sent += one
     arrive(last_copies)

time: 48 us -> 46.8 us (0.975)
  Pallas kernels: 47.3 us -> 46 us
    pallas_call x1, Pallas kernels: 45.9 us -> 44.7 us  [per_device(): pl.pallas_call(functools.partial(step_kernel, sizes), out_shape=(*outs[:2...]
where the time goes in v7:
time: 46.8 us; the launch traced here: 46.7 us
  Pallas kernels  46 us (98%)
  between operations  0.64 us (1%)
    pallas_call x1, Pallas kernels, per_device(): pl.pallas_call(functools.partial(step_kernel, sizes), out_shape=(*outs[:2...  44.7 us
    pallas_call x1, Pallas kernels, per_device(): pl.pallas_call(put_kernel, out_shape=outs, in_specs=[anywhere] * 4, out_s...  1.33 us

profile of v7, /device:TPU:1, one launch (start us, length us, event | category | flops | bytes accessed | tf_op | source)
XLA Modules:
  0.0 46.7 jit_solution(6524683056594296473)
XLA Ops:
  0.6 44.7 %step.1 = (bf16[4,4096]{1,0:T(4,128)(2,1)S(1)}, bf16[4,4096]{1,0:T(4,128)(2,1)S(1)}, f32[28,64,64]{2,1,0:T(8,128)S(1)}, f32[28,64,64]{2,1,0:T(8,128)S(1)}) custom-call(bf16[4,4096]{1,0:T(4,128)(2,1)} %bitcast.10, bf16[4,4096]{1,0:T(4,128)(2,1)} %bitcast.11, s32[4,27]{1,0:T(4,128)} %bitcast.13, s32[4,1728]{1,0:T(4,128)} %bitcast.12, ...), custom_call_target="tpu_custom_call" | custom-call | tf_op jit(solution)/shard_map/step/pallas_call | solution.py:608
  45.3 1.3 %put.1 = (bf16[4,4096]{1,0:T(4,128)(2,1)}, bf16[4,4096]{1,0:T(4,128)(2,1)}, f32[27,64,64]{2,1,0:T(8,128)}, f32[27,64,64]{2,1,0:T(8,128)}) custom-call(bf16[4,4096]{1,0:T(4,128)(2,1)S(1)} %get-tuple-element.12.refs_0_, bf16[4,4096]{1,0:T(4,128)(2,1)S(1)} %get-tuple-element.13.refs_1_, f32[28,64,64]{2,1,0:T(8,128)S(1)} %get-tuple-element.14.refs_2_, ...), custom_call_target="tpu_custom_call" | custom-call | tf_op jit(solution)/shard_map/put/pallas_call | solution.py:631

commit v8 on v7

--- a/solution.py
+++ b/solution.py
@@ -81,6 +81,14 @@
     deep_recv,
     relay,
 ):
+    loads = {}
+
+    def load(name, src, dst):
+        loads[name] = pltpu.make_async_copy(src, dst, load_sem.at[len(loads)])
+        loads[name].start()
+
+    load("x", x_hbm, x_ref)
+    load("ct", ct_hbm, ct_ref)
     n_x, n_y, n_z = sizes
     deep = n_z // ZPAR
     space = n_y * n_z
@@ -144,19 +152,10 @@
             src_ref=src, dst_ref=dst, send_sem=send, recv_sem=recv, device_id=target, device_id_type=MESH
         )
 
-    loads = {}
-    for i, (name, src, dst) in enumerate(
-        (
-            ("vox", vox_hbm, vox_ref),
-            ("src", src_hbm, src_ref),
-            ("x", x_hbm, x_ref),
-            ("ct", ct_hbm, ct_ref),
-            ("w2", w2_hbm, w2_ref),
-            ("w1", w1_hbm, w1_ref),
-        )
-    ):
-        loads[name] = pltpu.make_async_copy(src, dst, load_sem.at[i])
-        loads[name].start()
+    load("vox", vox_hbm, vox_ref)
+    load("src", src_hbm, src_ref)
+    load("w2", w2_hbm, w2_ref)
+    load("w1", w1_hbm, w1_ref)
 
     def iota(shape, dim):
         return lax.broadcasted_iota(jnp.int32, shape, dim)
@@ -275,18 +274,11 @@
             fill(table, ref[i], blocks + 2 * i)
 
     def pick(table, picked):
-        def one(g, carry):
-            for i in range(group_of):
-                k = g * group_of + i
-                for p in range(blocks // 2):
-                    lanes = slice(p * 2 * V, (p + 1) * 2 * V)
-                    both = jnp.where(
-                        low16, table[slots[k * blocks + 2 * p]], table[slots[k * blocks + 2 * p + 1]]
-                    )
-                    picked[k, :, lanes] = mxu(both, hot(spot_pair, pair_rows[k, :, lanes])).astype(BF16)
-            return carry
-
-        lax.fori_loop(0, K // group_of, one, 0)
+        for k in range(K):
+            for p in range(blocks // 2):
+                lanes = slice(p * 2 * V, (p + 1) * 2 * V)
+                both = jnp.where(low16, table[slots[k * blocks + 2 * p]], table[slots[k * blocks + 2 * p + 1]])
+                picked[k, :, lanes] = mxu(both, hot(spot_pair, pair_rows[k, :, lanes])).astype(BF16)
 
     def convolved(wt, picked):
         return mxu(wt[...], picked[...].reshape(K * C, n))
@@ -371,6 +363,8 @@
     loads["x"].wait()
     feat = to_channels(x_ref)
     feat_ref[...] = feat
+    loads["ct"].wait()
+    cot = to_channels(ct_ref)
     pl.semaphore_wait(barrier, len(near))
     feat_copies = to_neighbours(0, feat_ref.at[:, 0:half], feat_ref.at[:, half:n], halo_in)
     relay_signal(0)
@@ -379,8 +373,6 @@
     loads["vox"].wait()
     loads["src"].wait()
     make_rows()
-    loads["ct"].wait()
-    cot = to_channels(ct_ref)
     spread_out(cot, 1)
     loads["w2"].wait()
     pair_weights()

time: 46.8 us -> 46.6 us (level)
  no operation moved by 1% of the time
where the time goes in v8:
time: 46.6 us; the launch traced here: 46.4 us
  Pallas kernels  45.8 us (98%)
  between operations  0.64 us (1%)
    pallas_call x1, Pallas kernels, per_device(): pl.pallas_call(functools.partial(step_kernel, sizes), out_shape=(*outs[:2...  44.4 us
    pallas_call x1, Pallas kernels, per_device(): pl.pallas_call(put_kernel, out_shape=outs, in_specs=[anywhere] * 4, out_s...  1.33 us

profile of v8, /device:TPU:1, one launch (start us, length us, event | category | flops | bytes accessed | tf_op | source)
XLA Modules:
  0.0 46.4 jit_solution(18377112396066855494)
XLA Ops:
  0.6 44.4 %step.1 = (bf16[4,4096]{1,0:T(4,128)(2,1)S(1)}, bf16[4,4096]{1,0:T(4,128)(2,1)S(1)}, f32[28,64,64]{2,1,0:T(8,128)S(1)}, f32[28,64,64]{2,1,0:T(8,128)S(1)}) custom-call(bf16[4,4096]{1,0:T(4,128)(2,1)} %bitcast.10, bf16[4,4096]{1,0:T(4,128)(2,1)} %bitcast.11, s32[4,27]{1,0:T(4,128)} %bitcast.13, s32[4,1728]{1,0:T(4,128)} %bitcast.12, ...), custom_call_target="tpu_custom_call" | custom-call | tf_op jit(solution)/shard_map/step/pallas_call | solution.py:600
  45.1 1.3 %put.1 = (bf16[4,4096]{1,0:T(4,128)(2,1)}, bf16[4,4096]{1,0:T(4,128)(2,1)}, f32[27,64,64]{2,1,0:T(8,128)}, f32[27,64,64]{2,1,0:T(8,128)}) custom-call(bf16[4,4096]{1,0:T(4,128)(2,1)S(1)} %get-tuple-element.12.refs_0_, bf16[4,4096]{1,0:T(4,128)(2,1)S(1)} %get-tuple-element.13.refs_1_, f32[28,64,64]{2,1,0:T(8,128)S(1)} %get-tuple-element.14.refs_2_, ...), custom_call_target="tpu_custom_call" | custom-call | tf_op jit(solution)/shard_map/put/pallas_call | solution.py:623

commit v9 on v8

--- a/solution.py
+++ b/solution.py
@@ -347,6 +347,42 @@
             copies.append(remote(src_of(member(xx, yy, zz)), dst, send, recv, target))
         return [Batch(copies, send, recv, all_of, all_of)]
 
+    owners = -(-pad // per)
+
+    class Gather:
+        def __init__(self, which, mine):
+            send, recv = group_send.at[1, which], group_recv.at[1, which]
+
+            def some(count):
+                ref = sums.at[which, core, 0 : count * per]
+                return remote(ref, ref, send, recv, twin)
+
+            self.out, self.few, self.many = some(len(offsets)), some(owners - 1), some(owners)
+            copies = []
+            for dx, dy, dz in offsets:
+                xx, yy, zz = (x + dx) % n_x, (y + dy) % n_y, (z_par + dz) % ZPAR
+                target = (((z // ZPAR) * ZPAR + zz) * n_y + yy, xx * CORES + core)
+                copies.append(remote(mine, mine, send, recv, target))
+
+            @pl.when(me < owners)
+            def _():
+                for copy in copies:
+                    copy.start()
+
+        def wait_recv(self):
+            @pl.when(me < owners)
+            def _():
+                self.few.wait_recv()
+
+            @pl.when(me >= owners)
+            def _():
+                self.many.wait_recv()
+
+        def wait_send(self):
+            @pl.when(me < owners)
+            def _():
+                self.out.wait_send()
+
     def to_depths(which, src, dst):
         send, recv = deep_send.at[which], deep_recv.at[which]
         copies = []
@@ -437,8 +473,7 @@
         arrive(copies)
         sums[which, core, pl.ds(me * per, per)] = added(got3, which, deep)
         mine = mine_of(which)
-        every = sums.at[which, core, 0 : len(offsets) * per]
-        return to_members(1, which, lambda other: mine, mine, every)
+        return [Gather(which, mine)]
 
     def gather_pair(which, copies):
         arrive(copies)

time: 46.6 us -> 46.1 us (0.989)
  no operation moved by 1% of the time
where the time goes in v9:
time: 46.1 us; the launch traced here: 46 us
  Pallas kernels  45.4 us (98%)
  between operations  0.64 us (1%)
    pallas_call x1, Pallas kernels, per_device(): pl.pallas_call(functools.partial(step_kernel, sizes), out_shape=(*outs[:2...  44 us
    pallas_call x1, Pallas kernels, per_device(): pl.pallas_call(put_kernel, out_shape=outs, in_specs=[anywhere] * 4, out_s...  1.33 us

profile of v9, /device:TPU:1, one launch (start us, length us, event | category | flops | bytes accessed | tf_op | source)
XLA Modules:
  0.0 46.0 jit_solution(17620665668715112474)
XLA Ops:
  0.6 44.0 %step.1 = (bf16[4,4096]{1,0:T(4,128)(2,1)S(1)}, bf16[4,4096]{1,0:T(4,128)(2,1)S(1)}, f32[28,64,64]{2,1,0:T(8,128)S(1)}, f32[28,64,64]{2,1,0:T(8,128)S(1)}) custom-call(bf16[4,4096]{1,0:T(4,128)(2,1)} %bitcast.10, bf16[4,4096]{1,0:T(4,128)(2,1)} %bitcast.11, s32[4,27]{1,0:T(4,128)} %bitcast.13, s32[4,1728]{1,0:T(4,128)} %bitcast.12, ...), custom_call_target="tpu_custom_call" | custom-call | tf_op jit(solution)/shard_map/step/pallas_call | solution.py:635
  44.7 1.3 %put.1 = (bf16[4,4096]{1,0:T(4,128)(2,1)}, bf16[4,4096]{1,0:T(4,128)(2,1)}, f32[27,64,64]{2,1,0:T(8,128)}, f32[27,64,64]{2,1,0:T(8,128)}) custom-call(bf16[4,4096]{1,0:T(4,128)(2,1)S(1)} %get-tuple-element.12.refs_0_, bf16[4,4096]{1,0:T(4,128)(2,1)S(1)} %get-tuple-element.13.refs_1_, f32[28,64,64]{2,1,0:T(8,128)S(1)} %get-tuple-element.14.refs_2_, ...), custom_call_target="tpu_custom_call" | custom-call | tf_op jit(solution)/shard_map/put/pallas_call | solution.py:658

commit v10 on v9

--- a/solution.py
+++ b/solution.py
@@ -501,6 +501,7 @@
 
     one = reduce_pair(0)
     sent += one
+    spread(w1_ref, grad_pre)
     relay_wait(2)
     relay_signal(3)
     w2t[...] = w2_ref[...].T
@@ -512,7 +513,6 @@
     two = reduce_pair(1)
     sent += two
 
-    spread(w1_ref, grad_pre)
     two = scatter_reduce(1, two)
     sent += two
     rim = scattered(n).astype(BF16)

time: 46.1 us -> 46.2 us (level)
  no operation moved by 1% of the time
where the time goes in v10:
time: 46.2 us; the launch traced here: 46.1 us
  Pallas kernels  45.4 us (98%)
  between operations  0.64 us (1%)
    pallas_call x1, Pallas kernels, per_device(): pl.pallas_call(functools.partial(step_kernel, sizes), out_shape=(*outs[:2...  44.1 us
    pallas_call x1, Pallas kernels, per_device(): pl.pallas_call(put_kernel, out_shape=outs, in_specs=[anywhere] * 4, out_s...  1.33 us

profile of v10, /device:TPU:1, one launch (start us, length us, event | category | flops | bytes accessed | tf_op | source)
XLA Modules:
  0.0 46.1 jit_solution(9336088663478542464)
XLA Ops:
  0.6 44.1 %step.1 = (bf16[4,4096]{1,0:T(4,128)(2,1)S(1)}, bf16[4,4096]{1,0:T(4,128)(2,1)S(1)}, f32[28,64,64]{2,1,0:T(8,128)S(1)}, f32[28,64,64]{2,1,0:T(8,128)S(1)}) custom-call(bf16[4,4096]{1,0:T(4,128)(2,1)} %bitcast.10, bf16[4,4096]{1,0:T(4,128)(2,1)} %bitcast.11, s32[4,27]{1,0:T(4,128)} %bitcast.13, s32[4,1728]{1,0:T(4,128)} %bitcast.12, ...), custom_call_target="tpu_custom_call" | custom-call | tf_op jit(solution)/shard_map/step/pallas_call | solution.py:635
  44.7 1.3 %put.1 = (bf16[4,4096]{1,0:T(4,128)(2,1)}, bf16[4,4096]{1,0:T(4,128)(2,1)}, f32[27,64,64]{2,1,0:T(8,128)}, f32[27,64,64]{2,1,0:T(8,128)}) custom-call(bf16[4,4096]{1,0:T(4,128)(2,1)S(1)} %get-tuple-element.12.refs_0_, bf16[4,4096]{1,0:T(4,128)(2,1)S(1)} %get-tuple-element.13.refs_1_, f32[28,64,64]{2,1,0:T(8,128)S(1)} %get-tuple-element.14.refs_2_, ...), custom_call_target="tpu_custom_call" | custom-call | tf_op jit(solution)/shard_map/put/pallas_call | solution.py:658
